TPU v7x, 512 devices: a whole 4x8x8 slice. The times are simulated.
512 devices in a mesh: nodes: 128 (over y, z, core), feat: 4 (over x).
Axes of the slice: x: 4, y: 8, z: 8, core: 2. Of those that a mesh axis runs over, the one named last changes fastest.
Arguments:
- feats: bfloat16 [1536, 4, 8192], P('nodes', 'feat'), may hold values from -120 to 120
- w_qkv: bfloat16 [256, 768], P(None, 'feat'), may hold values from -0.375 to 0.375
- w_gcn: bfloat16 [256, 256], P(None, 'feat'), may hold values from -0.375 to 0.375
- nbr_owner: int32 [1536, 4], P('nodes'), may hold values from 0 to 127, all different within a row; in each aligned block of 12 rows (0 to 11, 12 to 23, ...) at most 2 rows name the same one
- nbr_tile: int32 [1536, 4], P('nodes'), may hold values from 0 to 11
- adj_blocks: bfloat16 [1536, 4, 128, 128], P('nodes', 'feat'), may hold values from -0.25 to 0.25
- grad_out: bfloat16 [1536, 4, 8192], P('nodes', 'feat'), may hold values from -6 to 6
Outputs:
- mixed: bfloat16 [1536, 4, 8192], P('nodes', 'feat')
- grad_x: bfloat16 [1536, 4, 8192], P('nodes', 'feat')
- grad_qkv: float32 [256, 768], P(None, 'feat')
- grad_gcn: float32 [256, 256], P(None, 'feat')
Inputs may be any that keep to these rules, and one draw needn't show every extreme that they name: `nbr_owner`: the 4 owners listed for one tile differ; the 12 tiles of one partition list one owner at most 2 times, and some partition lists some owner exactly 2 times.
All inputs are finite; a program needn't handle non-finite values.
Results may differ from a plain program's by a relative error of at most 0.012.
Values may be sent and summed in bfloat16 or wider, within the bound.
A program may use at most 64 MiB of HBM per device.

v0:
```python
import jax
import jax.numpy as jnp
from jax import lax
from jax.sharding import PartitionSpec as P

epsilon = 1e-06


def contract_rows(left, right):
    return lax.dot_general(
        left, right, (((0,), (0,)), ((), ())), preferred_element_type=jnp.float32
    )


def local(feats, w_qkv, w_gcn, nbr_owner, nbr_tile, adj_blocks, grad_out):
    tile_count = nbr_owner.shape[0]
    list_width = nbr_owner.shape[1]
    head_width = w_gcn.shape[1]
    tile_rows_n = feats.shape[2] // head_width
    row_count = tile_count * tile_rows_n
    gathered = lax.all_gather(feats, "feat", axis=1, tiled=True)
    head_count = gathered.shape[1]
    full_rows = (
        gathered.reshape(tile_count, head_count, tile_rows_n, head_width)
        .transpose(0, 2, 1, 3)
        .reshape(row_count, head_count * head_width)
    )
    adj_all = lax.all_gather(adj_blocks, "feat", axis=1, tiled=True)
    grad_rows = grad_out.reshape(row_count, head_width)
    node_count = lax.axis_size("nodes")
    slot_cap = max(2, (tile_count * list_width + node_count - 1) // node_count)
    total_rows = jnp.float32(row_count * node_count)
    proj = jnp.dot(full_rows, w_qkv, preferred_element_type=jnp.float32).astype(jnp.bfloat16)
    query_rows = proj[:, :head_width]
    key_rows = proj[:, head_width : 2 * head_width]
    value_rows = proj[:, 2 * head_width :]
    query_full = query_rows.astype(jnp.float32)
    key_full = key_rows.astype(jnp.float32)
    value_full = value_rows.astype(jnp.float32)
    sq_local = jnp.sum(query_full * query_full)
    sk_local = jnp.sum(key_full * key_full)
    kv_local = contract_rows(key_rows, value_rows)
    grad_full = grad_rows.astype(jnp.float32)
    kv_state, sq_sum, sk_sum = lax.psum((kv_local, sq_local, sk_local), "nodes")
    mix_rows = jnp.dot(query_full, kv_state, precision=lax.Precision.HIGHEST)
    pq_local = contract_rows(query_rows, grad_rows)
    pq_state, scale_grad = lax.psum((pq_local, jnp.sum(grad_full * mix_rows)), "nodes")
    attn_scale = jnp.sqrt(total_rows) / jnp.sqrt(sq_sum * sk_sum + epsilon)
    y_rows = jnp.dot(full_rows, w_gcn, preferred_element_type=jnp.float32).astype(jnp.bfloat16)
    owners = nbr_owner.reshape(-1)
    local_ids = nbr_tile.reshape(-1)
    owner_hot = (owners[:, None] == jnp.arange(node_count, dtype=jnp.int32)[None, :]).astype(
        jnp.int32
    )
    rank_within = jnp.sum((jnp.cumsum(owner_hot, axis=0) - owner_hot) * owner_hot, axis=1)
    slot_index = owners * slot_cap + rank_within
    request = jnp.zeros((node_count * slot_cap,), jnp.int32).at[slot_index].set(local_ids)
    incoming = lax.all_to_all(
        request.reshape(node_count, slot_cap), "nodes", split_axis=0, concat_axis=0, tiled=True
    )
    incoming_flat = incoming.reshape(-1)
    y_tiles = y_rows.reshape(tile_count, tile_rows_n * head_width)
    picked = jnp.take(y_tiles, incoming_flat, axis=0).reshape(
        node_count, slot_cap, tile_rows_n * head_width
    )
    fetched = lax.all_to_all(picked, "nodes", split_axis=0, concat_axis=0, tiled=True)
    neighbours = jnp.take(
        fetched.reshape(node_count * slot_cap, tile_rows_n * head_width), slot_index, axis=0
    )
    neighbours = neighbours.reshape(tile_count, list_width, tile_rows_n, head_width)
    gcn_sum = jnp.einsum(
        "tnab,tnbh->tah", adj_all, neighbours, preferred_element_type=jnp.float32
    ).reshape(row_count, head_width)
    mixed = (value_full + attn_scale * mix_rows + y_rows.astype(jnp.float32) + gcn_sum).astype(
        jnp.bfloat16
    )
    dm_state = attn_scale * pq_state
    denominator = sq_sum * sk_sum + epsilon
    gq_coef = -0.5 * scale_grad * attn_scale * sk_sum / denominator
    gk_coef = -0.5 * scale_grad * attn_scale * sq_sum / denominator
    dq_rows = (
        attn_scale * jnp.dot(grad_full, kv_state.T, precision=lax.Precision.HIGHEST)
        + 2.0 * gq_coef * query_full
    )
    dk_rows = (
        jnp.dot(value_full, dm_state.T, precision=lax.Precision.HIGHEST) + 2.0 * gk_coef * key_full
    )
    dv_rows = grad_full + jnp.dot(key_full, dm_state, precision=lax.Precision.HIGHEST)
    dqkv = jnp.concatenate([dq_rows, dk_rows, dv_rows], axis=1).astype(jnp.bfloat16)
    grad_tiles = grad_rows.reshape(tile_count, tile_rows_n, head_width)
    back_term = jnp.einsum(
        "tnab,tah->tnbh", adj_all, grad_tiles, preferred_element_type=jnp.float32
    ).astype(jnp.bfloat16)
    outgoing = jnp.zeros((node_count * slot_cap, tile_rows_n * head_width), jnp.bfloat16)
    outgoing = outgoing.at[slot_index].set(
        back_term.reshape(tile_count * list_width, tile_rows_n * head_width)
    )
    returned = lax.all_to_all(
        outgoing.reshape(node_count, slot_cap, tile_rows_n * head_width),
        "nodes",
        split_axis=0,
        concat_axis=0,
        tiled=True,
    )
    tile_hot = (incoming_flat[:, None] == jnp.arange(tile_count, dtype=jnp.int32)[None, :]).astype(
        jnp.bfloat16
    )
    back_sum = contract_rows(
        tile_hot, returned.reshape(node_count * slot_cap, tile_rows_n * head_width)
    )
    dy_rows = (grad_full + back_sum.reshape(row_count, head_width)).astype(jnp.bfloat16)
    qkv_local = contract_rows(full_rows, dqkv)
    gcn_local = contract_rows(full_rows, dy_rows)
    grad_qkv, grad_gcn = lax.psum((qkv_local, gcn_local), "nodes")
    partial_grad = lax.dot_general(
        dqkv, w_qkv, (((1,), (1,)), ((), ())), preferred_element_type=jnp.float32
    )
    partial_grad = partial_grad + lax.dot_general(
        dy_rows, w_gcn, (((1,), (1,)), ((), ())), preferred_element_type=jnp.float32
    )
    grad_x = lax.psum_scatter(
        partial_grad.astype(jnp.bfloat16), "feat", scatter_dimension=1, tiled=True
    )
    mixed_tiles = mixed.reshape(tile_count, 1, tile_rows_n * head_width)
    grad_x_tiles = grad_x.reshape(tile_count, 1, tile_rows_n * head_width)
    return (mixed_tiles, grad_x_tiles, grad_qkv, grad_gcn)


def solution(mesh):
    in_specs = (
        P("nodes", "feat", None),
        P(None, "feat"),
        P(None, "feat"),
        P("nodes", None),
        P("nodes", None),
        P("nodes", "feat", None, None),
        P("nodes", "feat", None),
    )
    out_specs = (
        P("nodes", "feat", None),
        P("nodes", "feat", None),
        P(None, "feat"),
        P(None, "feat"),
    )
    return jax.shard_map(local, mesh=mesh, in_specs=in_specs, out_specs=out_specs, check_vma=False)
```

profile of v0, /device:TPU:1, one launch (start us, length us, event | category | flops | bytes accessed | tf_op | source)
XLA Modules:
  0.0 1508.8 jit_solution(16477897437753999971)
XLA Ops:
  11.6 18.4 %all-to-all-start = ((s32[128,1,2]{2,1,0:T(1,128)}), s32[128,1,2]{2,1,0:T(1,128)S(1)}, u32[]{:S(2)}, u32[]{:S(2)}) async-start(s32[128,1,2]{2,1,0:T(1,128)} %bitcast.3), calls=%async_computation | async-start | bytes 131072 | tf_op jit(solution)/shard_map/all_to_all | solution.py:58
  31.4 16.1 %all-gather.2.cloned.1.call-done = bf16[12,4,128,128]{3,2,1,0:T(8,128)(2,1)} async-done(((bf16[12,1,128,128]{3,2,1,0:T(8,128)(2,1)}), bf16[12,4,128,128]{3,2,1,0:T(8,128)(2,1)}) %all-gather.2.cloned.1.call-update) | async-done | bytes 1572880 | tf_op jit(solution)/shard_map/all_gather | solution.py:28
  47.5 1.8 convolution_convert_fusion.2
  51.5 4.4 scatter_custom_fusion.1
  55.9 7.6 reshape.166
  63.5 14.9 all-to-all-start.2
  78.4 12.6 all_gather.6
  96.4 5.2 gather_fusion
  101.5 7.6 gather.13
  109.2 8.0 broadcast_select_fusion
  117.2 56.8 %all-to-all-done.2 = bf16[128,2,8192]{2,1,0:T(2,128)(2,1)} async-done(((bf16[128,2,8192]{2,1,0:T(2,128)(2,1)}), bf16[128,2,8192]{2,1,0:T(2,128)(2,1)}, u32[]{:S(2)}, u32[]{:S(2)}) %all-to-all-start.2) | async-done | bytes 4194336 | tf_op jit(solution)/shard_map/all_to_all | solution.py:98
  174.0 17.7 %all-to-all-start.1 = ((bf16[128,2,8192]{2,1,0:T(2,128)(2,1)}), bf16[128,2,8192]{2,1,0:T(2,128)(2,1)}, u32[]{:S(2)}, u32[]{:S(2)}) async-start(bf16[128,2,8192]{2,1,0:T(2,128)(2,1)} %broadcast_select_fusion), calls=%async_computation.1 | async-start | bytes 8388608 | tf_op jit(solution)/shard_map/all_to_all | solution.py:66
  193.1 572.0 %psum.51 = f32[64,64]{1,0:T(8,128)S(1)} all-reduce(f32[64,64]{1,0:T(8,128)S(1)} %fusion.29), channel_id=1, replica_groups=mesh['nodes'=128,'feat'=4] {'nodes'}, use_global_device_ids=true, to_apply=%region_4.0 | all-reduce | flops 4096 | bytes 32768 | tf_op jit(solution)/shard_map/psum | solution.py:44
  766.1 1.7 fusion.22
  767.8 490.9 %all-reduce = (f32[]{:T(128)}, f32[]{:T(128)}, f32[64,64]{1,0:T(8,128)S(1)}, f32[]{:T(128)}) all-reduce(f32[]{:T(128)} %get-tuple-element.5, f32[]{:T(128)} %get-tuple-element.4, f32[64,64]{1,0:T(8,128)S(1)} %fusion.34, f32[]{:T(128)} %get-tuple-element.12), channel_id=1, replica_groups=mesh['nodes'=128,'feat'=4] {'nodes'}, use_global_device_ids=true, to_apply=%region_1.0 | all-reduce | flops 4099 | bytes 32792 | tf_op jit(solution)/shard_map/psum | solution.py:44
  1265.0 7.2 reshape.167
  1272.2 3.7 fusion.19
  1276.5 2.8 fusion
  1280.6 7.2 reshape.160
  1287.8 4.5 gather_fusion.1
  1292.3 2.6 gather.15
  1294.9 2.7 fusion.11
  1300.4 5.1 reduce-scatter.2.cloned.1.call-done
  1307.8 191.4 %all-reduce.4.cloned.1.call-done = (f32[256,192]{0,1:T(8,128)}, f32[256,64]{0,1:T(8,128)}) async-done(((f32[256,192]{0,1:T(8,128)}, f32[256,64]{0,1:T(8,128)}), (f32[256,192]{0,1:T(8,128)}, f32[256,64]{0,1:T(8,128)})) %all-reduce.4.cloned.1.call-update) | async-done | bytes 262160 | tf_op jit(solution)/shard_map/psum | solution.py:114
  (85 shorter events, 28.2 us)
Async XLA Ops:
  7.2 185.4 %copy-start = (bf16[256,192]{0,1:T(8,128)(2,1)S(1)}, bf16[256,192]{0,1:T(8,128)(2,1)}, u32[]{:S(2)}) copy-start(bf16[256,192]{0,1:T(8,128)(2,1)} %param.8) | copy-start | bytes 294916
  7.2 40.3 %all-gather.2.cloned.1.call-start = ((), (), s32[]{:S(2)}) async-start(), calls=%async_computation.4 | async-start | bytes 1966080 | tf_op jit(solution)/shard_map/all_gather | solution.py:28
  11.6 52.0 %all-to-all-start = ((s32[128,1,2]{2,1,0:T(1,128)}), s32[128,1,2]{2,1,0:T(1,128)S(1)}, u32[]{:S(2)}, u32[]{:S(2)}) async-start(s32[128,1,2]{2,1,0:T(1,128)} %bitcast.3), calls=%async_computation | async-start | bytes 131072 | tf_op jit(solution)/shard_map/all_to_all | solution.py:58
  63.5 14.9 copy-start.8
  63.5 110.4 %all-to-all-start.2 = ((bf16[128,2,8192]{2,1,0:T(2,128)(2,1)}), bf16[128,2,8192]{2,1,0:T(2,128)(2,1)}, u32[]{:S(2)}, u32[]{:S(2)}) async-start(bf16[128,2,8192]{2,1,0:T(2,128)(2,1)} %reshape.166), calls=%async_computation.2 | async-start | bytes 8388608 | tf_op jit(solution)/shard_map/all_to_all | solution.py:98
  92.9 1.1 copy-start.11
  117.2 74.8 %copy-start.1 = (bf16[12,1,8192]{2,0,1:T(8,128)(2,1)S(1)}, bf16[12,1,8192]{2,0,1:T(8,128)(2,1)}, u32[]{:S(2)}) copy-start(bf16[12,1,8192]{2,0,1:T(8,128)(2,1)} %param.13) | copy-start | bytes 589828
  174.0 1106.6 %all-to-all-start.1 = ((bf16[128,2,8192]{2,1,0:T(2,128)(2,1)}), bf16[128,2,8192]{2,1,0:T(2,128)(2,1)}, u32[]{:S(2)}, u32[]{:S(2)}) async-start(bf16[128,2,8192]{2,1,0:T(2,128)(2,1)} %broadcast_select_fusion), calls=%async_computation.1 | async-start | bytes 8388608 | tf_op jit(solution)/shard_map/all_to_all | solution.py:66
  191.7 1113.9 %reduce-scatter.2.cloned.1.call-start = ((), (), s32[]{:S(2)}) async-start(), calls=%async_computation.5 | async-start | bytes 983040 | tf_op jit(solution)/shard_map/reduce_scatter | solution.py:121
  1262.3 0.9 copy-start.9
  1262.7 2.3 copy-start.4
  1263.3 1.7 copy-start.6
  1276.5 3.0 copy-start.5
  1276.5 3.0 copy-start.7
  1276.5 3.0 copy-start.10
  1279.3 219.9 %all-reduce.4.cloned.1.call-start = ((), (), s32[]{:S(2)}) async-start(), calls=%async_computation.6 | async-start | bytes 524288 | tf_op jit(solution)/shard_map/psum | solution.py:114
  1294.9 2.7 copy-start.3
  1297.6 1.4 copy-start.2
Sparse Core Ops, SparseCore 0:
  10.1 37.3 all-gather.1
  1279.4 26.0 reduce-scatter.1
  1309.4 189.6 all-reduce.3
where the time goes:
time: 1510 us
  blocking collectives  1080 us (72%)
  waiting for transfers between devices  270 us (18%)
  local copies, waits for them, and re-layouts  65.7 us (4%)
  starting transfers between devices  51.4 us (3%)
  matrix products  18.5 us (1%)
  between operations  17.6 us (1%)
    psum x2, blocking collectives, local(): kv_state, sq_sum, sk_sum = lax.psum((kv_local, sq_local, sk_local), 'nodes')  1060 us
    psum x1, waiting for transfers between devices, local(): grad_qkv, grad_gcn = lax.psum((qkv_local, gcn_local), 'nodes')  191 us
    all_to_all x1, waiting for transfers between devices, local(): lax.all_to_all(outgoing.reshape(node_count, slot_cap, tile_rows_n * head_...  56.8 us
  transfers between devices with their start and end apart: 6, of which 4 were waited for; matrix products, arithmetic and copies ran while one was open for 6% of the time, Pallas kernels for 0%

commit v1 on v0

v1 whole, which is shorter than its diff:
```python
import functools

import jax
import jax.numpy as jnp
from jax import lax
from jax.experimental import pallas as pl
from jax.experimental.pallas import tpu as pltpu
from jax.sharding import PartitionSpec as P

epsilon = 1e-06
HIGHEST = lax.Precision.HIGHEST
SIDE = 8


def contract_rows(left, right):
    return lax.dot_general(
        left, right, (((0,), (0,)), ((), ())), preferred_element_type=jnp.float32
    )


def sum_kernel(
    x_ref, o_ref, core_buf, half_buf, y_buf, piece_buf, z_buf, total, send_core, recv_core,
    send_y, recv_y, send_z, recv_z, send_g, recv_g, send_last, recv_last,
):
    rows = x_ref.shape[0]
    half = rows // 2
    piece = half // SIDE
    me = lax.axis_index("nodes")
    core = lax.rem(me, 2)
    z = lax.rem(me // 2, SIDE)
    y = me // (2 * SIDE)
    partner = me + 1 - 2 * core

    def at_y(k):
        other = lax.rem(y + k, SIDE)
        return other, (other * SIDE + z) * 2 + core

    def at_z(k):
        other = lax.rem(z + k, SIDE)
        return other, (y * SIDE + other) * 2 + core

    barrier = pltpu.get_barrier_semaphore()
    pl.semaphore_signal(barrier, inc=1, device_id={"nodes": partner})
    for k in range(1, SIDE):
        pl.semaphore_signal(barrier, inc=1, device_id={"nodes": at_y(k)[1]})
        pl.semaphore_signal(barrier, inc=1, device_id={"nodes": at_z(k)[1]})
    pl.semaphore_wait(barrier, 2 * SIDE - 1)

    def block(start, size):
        return pl.ds(pl.multiple_of(start, 8), size)

    copies = []

    def send(src, dst, send_sem, recv_sem, target):
        copy = pltpu.make_async_remote_copy(
            src_ref=src, dst_ref=dst, send_sem=send_sem, recv_sem=recv_sem,
            device_id={"nodes": target},
        )
        copy.start()
        copies.append(copy)
        return copy

    first = send(
        x_ref.at[block((1 - core) * half, half)], core_buf, send_core, recv_core, partner
    )
    first.wait_recv()
    half_buf[...] = x_ref[block(core * half, half), :] + core_buf[...]

    stage = []
    for k in range(1, SIDE):
        other, target = at_y(k)
        stage.append(
            send(
                half_buf.at[block(other * piece, piece)], y_buf.at[y],
                send_y.at[k - 1], recv_y.at[k - 1], target,
            )
        )
    y_buf[y] = half_buf[block(y * piece, piece), :]
    for copy in stage:
        copy.wait_recv()
    acc = y_buf[0]
    for k in range(1, SIDE):
        acc = acc + y_buf[k]
    piece_buf[...] = acc

    stage = []
    for k in range(1, SIDE):
        other, target = at_z(k)
        stage.append(
            send(piece_buf, z_buf.at[z], send_z.at[k - 1], recv_z.at[k - 1], target)
        )
    z_buf[z] = acc
    for copy in stage:
        copy.wait_recv()
    acc = z_buf[0]
    for k in range(1, SIDE):
        acc = acc + z_buf[k]
    mine = block(core * half + y * piece, piece)
    total[mine, :] = acc

    stage = []
    for k in range(1, SIDE):
        other, target = at_y(k)
        stage.append(
            send(total.at[mine], total.at[mine], send_g.at[k - 1], recv_g.at[k - 1], target)
        )
    for copy in stage:
        copy.wait_recv()

    whole = block(core * half, half)
    last = send(total.at[whole], total.at[whole], send_last, recv_last, partner)
    last.wait_recv()
    for copy in copies:
        copy.wait_send()
    o_ref[...] = total[...]


def sum_nodes(x, collective_id):
    rows, lanes = x.shape
    half = rows // 2
    piece = half // SIDE
    f32 = jnp.float32
    dma = pltpu.SemaphoreType.DMA
    return pl.pallas_call(
        sum_kernel,
        out_shape=jax.ShapeDtypeStruct((rows, lanes), f32),
        in_specs=[pl.BlockSpec(memory_space=pltpu.VMEM)],
        out_specs=pl.BlockSpec(memory_space=pltpu.VMEM),
        scratch_shapes=[
            pltpu.VMEM((half, lanes), f32),
            pltpu.VMEM((half, lanes), f32),
            pltpu.VMEM((SIDE, piece, lanes), f32),
            pltpu.VMEM((piece, lanes), f32),
            pltpu.VMEM((SIDE, piece, lanes), f32),
            pltpu.VMEM((rows, lanes), f32),
            dma, dma,
            dma((SIDE - 1,)), dma((SIDE - 1,)),
            dma((SIDE - 1,)), dma((SIDE - 1,)),
            dma((SIDE - 1,)), dma((SIDE - 1,)),
            dma, dma,
        ],
        compiler_params=pltpu.CompilerParams(
            collective_id=collective_id, has_side_effects=True
        ),
        name="sum_nodes",
    )(x)


def local(feats, w_qkv, w_gcn, nbr_owner, nbr_tile, adj_blocks, grad_out):
    tile_count = nbr_owner.shape[0]
    list_width = nbr_owner.shape[1]
    head_width = w_gcn.shape[1]
    tile_rows_n = feats.shape[2] // head_width
    row_count = tile_count * tile_rows_n
    gathered = lax.all_gather(feats, "feat", axis=1, tiled=True)
    head_count = gathered.shape[1]
    full_rows = (
        gathered.reshape(tile_count, head_count, tile_rows_n, head_width)
        .transpose(0, 2, 1, 3)
        .reshape(row_count, head_count * head_width)
    )
    adj_all = lax.all_gather(adj_blocks, "feat", axis=1, tiled=True)
    grad_rows = grad_out.reshape(row_count, head_width)
    node_count = lax.axis_size("nodes")
    slot_cap = max(2, (tile_count * list_width + node_count - 1) // node_count)
    total_rows = jnp.float32(row_count * node_count)

    owners = nbr_owner.reshape(-1)
    local_ids = nbr_tile.reshape(-1)
    owner_hot = (owners[:, None] == jnp.arange(node_count, dtype=jnp.int32)[None, :]).astype(
        jnp.int32
    )
    rank_within = jnp.sum((jnp.cumsum(owner_hot, axis=0) - owner_hot) * owner_hot, axis=1)
    slot_index = owners * slot_cap + rank_within
    request = jnp.zeros((node_count * slot_cap,), jnp.int32).at[slot_index].set(local_ids)
    incoming = lax.all_to_all(
        request.reshape(node_count, slot_cap), "nodes", split_axis=0, concat_axis=0, tiled=True
    )
    incoming_flat = incoming.reshape(-1)

    grad_tiles = grad_rows.reshape(tile_count, tile_rows_n, head_width)
    back_term = jnp.einsum(
        "tnab,tah->tnbh", adj_all, grad_tiles, preferred_element_type=jnp.float32
    ).astype(jnp.bfloat16)
    outgoing = jnp.zeros((node_count * slot_cap, tile_rows_n * head_width), jnp.bfloat16)
    outgoing = outgoing.at[slot_index].set(
        back_term.reshape(tile_count * list_width, tile_rows_n * head_width)
    )
    returned = lax.all_to_all(
        outgoing.reshape(node_count, slot_cap, tile_rows_n * head_width),
        "nodes",
        split_axis=0,
        concat_axis=0,
        tiled=True,
    )

    proj = jnp.dot(full_rows, w_qkv, preferred_element_type=jnp.float32).astype(jnp.bfloat16)
    query_rows = proj[:, :head_width]
    key_rows = proj[:, head_width : 2 * head_width]
    value_rows = proj[:, 2 * head_width :]
    query_full = query_rows.astype(jnp.float32)
    key_full = key_rows.astype(jnp.float32)
    value_full = value_rows.astype(jnp.float32)
    grad_full = grad_rows.astype(jnp.float32)
    sq_local = jnp.sum(query_full * query_full)
    sk_local = jnp.sum(key_full * key_full)
    kv_local = contract_rows(key_rows, value_rows)
    pq_local = contract_rows(query_rows, grad_rows)
    stacked = jnp.concatenate([proj, grad_rows], axis=1)
    x_local = contract_rows(full_rows, stacked)
    depth = x_local.shape[0]
    lanes = 2 * head_width
    squares = jnp.concatenate(
        [
            jnp.broadcast_to(sq_local, (head_width // 2, lanes)),
            jnp.broadcast_to(sk_local, (head_width // 2, lanes)),
        ],
        axis=0,
    )
    sent = jnp.concatenate(
        [
            x_local[:, :lanes],
            x_local[:, lanes:],
            jnp.concatenate([kv_local, pq_local], axis=1),
            squares,
        ],
        axis=0,
    )
    summed = sum_nodes(sent, 0)
    x_query = summed[:depth, :head_width]
    x_key = summed[:depth, head_width:]
    x_value = summed[depth : 2 * depth, :head_width]
    x_grad = summed[depth : 2 * depth, head_width:]
    kv_state = summed[2 * depth : 2 * depth + head_width, :head_width]
    pq_state = summed[2 * depth : 2 * depth + head_width, head_width:]
    sq_sum = summed[2 * depth + head_width, 0]
    sk_sum = summed[2 * depth + head_width + head_width // 2, 0]
    scale_grad = jnp.sum(pq_state * kv_state)
    attn_scale = jnp.sqrt(total_rows) / jnp.sqrt(sq_sum * sk_sum + epsilon)
    dm_state = attn_scale * pq_state
    denominator = sq_sum * sk_sum + epsilon
    gq_coef = -0.5 * scale_grad * attn_scale * sk_sum / denominator
    gk_coef = -0.5 * scale_grad * attn_scale * sq_sum / denominator
    grad_qkv = jnp.concatenate(
        [
            attn_scale * jnp.dot(x_grad, kv_state.T, precision=HIGHEST)
            + 2.0 * gq_coef * x_query,
            jnp.dot(x_value, dm_state.T, precision=HIGHEST) + 2.0 * gk_coef * x_key,
            x_grad + jnp.dot(x_key, dm_state, precision=HIGHEST),
        ],
        axis=1,
    )

    y_rows = jnp.dot(full_rows, w_gcn, preferred_element_type=jnp.float32).astype(jnp.bfloat16)
    y_tiles = y_rows.reshape(tile_count, tile_rows_n * head_width)
    picked = (
        y_tiles.at[incoming_flat]
        .get(mode="promise_in_bounds")
        .reshape(node_count, slot_cap, tile_rows_n * head_width)
    )
    fetched = lax.all_to_all(picked, "nodes", split_axis=0, concat_axis=0, tiled=True)
    neighbours = (
        fetched.reshape(node_count * slot_cap, tile_rows_n * head_width)
        .at[slot_index]
        .get(mode="promise_in_bounds")
    )
    neighbours = neighbours.reshape(tile_count, list_width, tile_rows_n, head_width)
    gcn_sum = jnp.einsum(
        "tnab,tnbh->tah", adj_all, neighbours, preferred_element_type=jnp.float32
    ).reshape(row_count, head_width)
    mix_rows = jnp.dot(query_full, kv_state, precision=HIGHEST)
    mixed = (value_full + attn_scale * mix_rows + y_rows.astype(jnp.float32) + gcn_sum).astype(
        jnp.bfloat16
    )
    dq_rows = (
        attn_scale * jnp.dot(grad_full, kv_state.T, precision=HIGHEST)
        + 2.0 * gq_coef * query_full
    )
    dk_rows = jnp.dot(value_full, dm_state.T, precision=HIGHEST) + 2.0 * gk_coef * key_full
    dv_rows = grad_full + jnp.dot(key_full, dm_state, precision=HIGHEST)
    dqkv = jnp.concatenate([dq_rows, dk_rows, dv_rows], axis=1).astype(jnp.bfloat16)

    tile_hot = (incoming_flat[:, None] == jnp.arange(tile_count, dtype=jnp.int32)[None, :]).astype(
        jnp.bfloat16
    )
    back_sum = contract_rows(
        tile_hot, returned.reshape(node_count * slot_cap, tile_rows_n * head_width)
    )
    dy_rows = (grad_full + back_sum.reshape(row_count, head_width)).astype(jnp.bfloat16)
    gcn_local = contract_rows(full_rows, dy_rows)
    gcn_sent = jnp.concatenate([gcn_local[: depth // 2], gcn_local[depth // 2 :]], axis=1)
    gcn_summed = sum_nodes(gcn_sent, 1)
    grad_gcn = jnp.concatenate([gcn_summed[:, :head_width], gcn_summed[:, head_width:]], axis=0)
    partial_grad = lax.dot_general(
        dqkv, w_qkv, (((1,), (1,)), ((), ())), preferred_element_type=jnp.float32
    )
    partial_grad = partial_grad + lax.dot_general(
        dy_rows, w_gcn, (((1,), (1,)), ((), ())), preferred_element_type=jnp.float32
    )
    grad_x = lax.psum_scatter(
        partial_grad.astype(jnp.bfloat16), "feat", scatter_dimension=1, tiled=True
    )
    mixed_tiles = mixed.reshape(tile_count, 1, tile_rows_n * head_width)
    grad_x_tiles = grad_x.reshape(tile_count, 1, tile_rows_n * head_width)
    return (mixed_tiles, grad_x_tiles, grad_qkv, grad_gcn)


def solution(mesh):
    in_specs = (
        P("nodes", "feat", None),
        P(None, "feat"),
        P(None, "feat"),
        P("nodes", None),
        P("nodes", None),
        P("nodes", "feat", None, None),
        P("nodes", "feat", None),
    )
    out_specs = (
        P("nodes", "feat", None),
        P("nodes", "feat", None),
        P(None, "feat"),
        P(None, "feat"),
    )
    return jax.shard_map(local, mesh=mesh, in_specs=in_specs, out_specs=out_specs, check_vma=False)
```

time: 1510 us -> 399 us (0.26)
  blocking collectives: 1080 us -> 12.6 us
  waiting for transfers between devices: 270 us -> 80.2 us
  Pallas kernels: 0 us -> 137 us
    psum x2 -> x0, blocking collectives: 1060 us -> none  [local(): kv_state, sq_sum, sk_sum = lax.psum((kv_local, sq_local, sk_local), 'nodes')]
    psum x1 -> x0, waiting for transfers between devices: 191 us -> none  [local(): grad_qkv, grad_gcn = lax.psum((qkv_local, gcn_local), 'nodes')]
    pallas_call x0 -> x2, Pallas kernels: none -> 137 us  [sum_nodes(): pl.pallas_call(sum_kernel, out_shape=jax.ShapeDtypeStruct((rows, lanes),...]
  transfers between devices with their start and end apart: 6 -> 5, of which waited for: 4 -> 2; matrix products, arithmetic and copies ran while one was open for 6% -> 24% of each run, Pallas kernels for 0% -> 34%
where the time goes in v1:
time: 399 us; the launch traced here: 397 us
  Pallas kernels  137 us (34%)
  waiting for transfers between devices  80.2 us (20%)
  local copies, waits for them, and re-layouts  72.9 us (18%)
  starting transfers between devices  51.3 us (13%)
  matrix products  20.2 us (5%)
  between operations  17.9 us (4%)
  blocking collectives  12.6 us (3%)
  other arithmetic  5.03 us (1%)
    pallas_call x2, Pallas kernels, sum_nodes(): pl.pallas_call(sum_kernel, out_shape=jax.ShapeDtypeStruct((rows, lanes),...  137 us
    all_to_all x1, waiting for transfers between devices, local(): lax.all_to_all(outgoing.reshape(node_count, slot_cap, tile_rows_n * head_...  64.2 us
    all_to_all x1, starting transfers between devices, local(): lax.all_to_all(request.reshape(node_count, slot_cap), 'nodes', split_axis...  18.4 us
    all_to_all x1, starting transfers between devices, local(): lax.all_to_all(picked, 'nodes', split_axis=0, concat_axis=0, tiled=True)  17.7 us
    all_gather x1, waiting for transfers between devices, local(): adj_all = lax.all_gather(adj_blocks, 'feat', axis=1, tiled=True)  15.3 us
    all_to_all x1, starting transfers between devices, local(): lax.all_to_all(outgoing.reshape(node_count, slot_cap, tile_rows_n * head_...  14.9 us
    all_gather x1, blocking collectives, local(): gathered = lax.all_gather(feats, 'feat', axis=1, tiled=True)  12.6 us
  transfers between devices with their start and end apart: 5, of which 2 were waited for; matrix products, arithmetic and copies ran while one was open for 24% of the time, Pallas kernels for 34%

profile of v1, /device:TPU:1, one launch (start us, length us, event | category | flops | bytes accessed | tf_op | source)
XLA Modules:
  0.0 397.1 jit_solution(14472437882062523247)
XLA Ops:
  12.3 18.4 %all-to-all-start = ((s32[128,1,2]{2,1,0:T(1,128)}), s32[128,1,2]{2,1,0:T(1,128)S(1)}, u32[]{:S(2)}, u32[]{:S(2)}) async-start(s32[128,1,2]{2,1,0:T(1,128)} %bitcast.6), calls=%async_computation | async-start | bytes 131072 | tf_op jit(solution)/shard_map/all_to_all | solution.py:176
  30.8 1.4 reshape_reshape.3
  32.2 15.3 %all-gather.2.cloned.1.call-done = bf16[12,4,128,128]{3,2,1,0:T(8,128)(2,1)} async-done(((bf16[12,1,128,128]{3,2,1,0:T(8,128)(2,1)}), bf16[12,4,128,128]{3,2,1,0:T(8,128)(2,1)}) %all-gather.2.cloned.1.call-update) | async-done | bytes 1572880 | tf_op jit(solution)/shard_map/all_gather | solution.py:162
  47.5 1.8 convolution_convert_fusion.2
  51.5 4.4 %scatter_custom_fusion.1 = bf16[256,8192]{1,0:T(8,128)(2,1)} fusion(s32[48]{0:T(128)S(1)} %fusion.57, bf16[48,8192]{1,0:T(8,128)(2,1)S(1)} %reshape.170, bf16[]{:T(256)} %constant.26.clone.1), kind=kCustom, calls=%fused_computation.21 | custom fusion | bytes 4194306 | tf_op jit(solution)/shard_map/scatter | solution.py:186
  55.9 7.7 %reshape.137 = bf16[128,2,8192]{2,1,0:T(2,128)(2,1)} reshape(bf16[256,8192]{1,0:T(8,128)(2,1)} %scatter_custom_fusion.1) | data formatting | bytes 8388608 | tf_op jit(solution)/shard_map/reshape | solution.py:190
  63.6 14.9 %all-to-all-start.2 = ((bf16[128,2,8192]{2,1,0:T(2,128)(2,1)}), bf16[128,2,8192]{2,1,0:T(2,128)(2,1)}, u32[]{:S(2)}, u32[]{:S(2)}) async-start(bf16[128,2,8192]{2,1,0:T(2,128)(2,1)} %reshape.137), calls=%async_computation.2 | async-start | bytes 8388608 | tf_op jit(solution)/shard_map/all_to_all | solution.py:189
  78.5 12.6 %all_gather.6 = bf16[12,4,8192]{2,0,1:T(8,128)(2,1)S(1)} all-gather(bf16[12,1,8192]{2,0,1:T(8,128)(2,1)S(1)} %copy-done.10), channel_id=1, replica_groups=mesh['nodes'=128,'feat'=4] {'feat'}, dimensions={1}, use_global_device_ids=true | all-gather | bytes 983040 | tf_op jit(solution)/shard_map/all_gather | solution.py:155
  97.1 5.1 %gather_fusion = bf16[256,8192]{1,0:T(8,128)(2,1)} fusion(bf16[12,8192]{1,0:T(8,128)(2,1)S(1)} %reshape.128, s32[1024]{0:T(1024)S(1)} %pad_clamp_fusion.1), kind=kCustom, calls=%fused_computation | custom fusion | bytes 8389632 | tf_op jit(solution)/shard_map/gather | solution.py:258
  102.2 7.6 %reshape.131 = bf16[128,2,8192]{2,1,0:T(2,128)(2,1)} reshape(bf16[256,8192]{1,0:T(8,128)(2,1)} %gather_fusion) | data formatting | bytes 8388608 | tf_op jit(solution)/shard_map/reshape | solution.py:259
  109.8 64.2 %all-to-all-done.2 = bf16[128,2,8192]{2,1,0:T(2,128)(2,1)} async-done(((bf16[128,2,8192]{2,1,0:T(2,128)(2,1)}), bf16[128,2,8192]{2,1,0:T(2,128)(2,1)}, u32[]{:S(2)}, u32[]{:S(2)}) %all-to-all-start.2) | async-done | bytes 4194336 | tf_op jit(solution)/shard_map/all_to_all | solution.py:189
  174.0 17.7 %all-to-all-start.1 = ((bf16[128,2,8192]{2,1,0:T(2,128)(2,1)}), bf16[128,2,8192]{2,1,0:T(2,128)(2,1)}, u32[]{:S(2)}, u32[]{:S(2)}) async-start(bf16[128,2,8192]{2,1,0:T(2,128)(2,1)} %reshape.131), calls=%async_computation.1 | async-start | bytes 8388608 | tf_op jit(solution)/shard_map/all_to_all | solution.py:261
  196.7 115.3 %sum_nodes.2 = f32[640,128]{1,0:T(8,128)} custom-call(f32[640,128]{1,0:T(8,128)} %copy-done.9), custom_call_target="tpu_custom_call" | custom-call | tf_op jit(solution)/shard_map/sum_nodes/pallas_call | solution.py:124
  314.6 1.5 multiply_reduce_fusion
  327.2 7.2 %reshape.138 = bf16[256,8192]{1,0:T(8,128)(2,1)} reshape(bf16[128,2,8192]{2,1,0:T(2,128)(2,1)} %all-to-all-done.2) | data formatting | bytes 8388608 | tf_op jit(solution)/shard_map/reshape | solution.py:287
  334.4 3.7 fusion.26
  339.4 1.4 copy.58
  340.7 1.3 fusion
  342.1 7.2 %reshape.132 = bf16[256,8192]{1,0:T(8,128)(2,1)} reshape(bf16[128,2,8192]{2,1,0:T(2,128)(2,1)} %all-to-all-done.1) | data formatting | bytes 8388608 | tf_op jit(solution)/shard_map/reshape | solution.py:263
  349.3 5.4 %gather_fusion.1 = bf16[48,8192]{1,0:T(8,128)(2,1)} fusion(bf16[256,8192]{1,0:T(8,128)(2,1)} %reshape.132, s32[1024]{0:T(1024)S(1)} %pad_clamp_fusion), kind=kCustom, calls=%fused_computation.1 | custom fusion | bytes 1573056 | tf_op jit(solution)/shard_map/gather | solution.py:265
  354.7 3.5 reshape.133
  358.3 2.1 convolution_bitcast_fusion
  360.4 1.5 fusion.7
  364.7 21.6 %sum_nodes.3 = f32[128,128]{1,0:T(8,128)} custom-call(f32[128,128]{1,0:T(8,128)} %pad_maximum_fusion.2.x_ref), custom_call_target="tpu_custom_call" | custom-call | tf_op jit(solution)/shard_map/sum_nodes/pallas_call | solution.py:124
  (93 shorter events, 36.3 us)
Async XLA Ops:
  7.2 185.4 %copy-start = (bf16[256,192]{0,1:T(8,128)(2,1)S(1)}, bf16[256,192]{0,1:T(8,128)(2,1)}, u32[]{:S(2)}) copy-start(bf16[256,192]{0,1:T(8,128)(2,1)} %param.8) | copy-start | bytes 294916
  7.2 40.3 %all-gather.2.cloned.1.call-start = ((), (), s32[]{:S(2)}) async-start(), calls=%async_computation.4 | async-start | bytes 1966080 | tf_op jit(solution)/shard_map/all_gather | solution.py:162
  12.3 51.2 %all-to-all-start = ((s32[128,1,2]{2,1,0:T(1,128)}), s32[128,1,2]{2,1,0:T(1,128)S(1)}, u32[]{:S(2)}, u32[]{:S(2)}) async-start(s32[128,1,2]{2,1,0:T(1,128)} %bitcast.6), calls=%async_computation | async-start | bytes 131072 | tf_op jit(solution)/shard_map/all_to_all | solution.py:176
  63.6 14.9 %copy-start.10 = (bf16[12,1,8192]{2,0,1:T(8,128)(2,1)S(1)}, bf16[12,1,8192]{2,0,1:T(8,128)(2,1)}, u32[]{:S(2)}) copy-start(bf16[12,1,8192]{2,0,1:T(8,128)(2,1)} %param.7) | copy-start | bytes 589828
  63.6 110.4 %all-to-all-start.2 = ((bf16[128,2,8192]{2,1,0:T(2,128)(2,1)}), bf16[128,2,8192]{2,1,0:T(2,128)(2,1)}, u32[]{:S(2)}, u32[]{:S(2)}) async-start(bf16[128,2,8192]{2,1,0:T(2,128)(2,1)} %reshape.137), calls=%async_computation.2 | async-start | bytes 8388608 | tf_op jit(solution)/shard_map/all_to_all | solution.py:189
  92.9 1.1 copy-start.11
  94.3 0.7 copy-start.6
  109.8 82.2 %copy-start.3 = (bf16[12,1,8192]{2,0,1:T(8,128)(2,1)S(1)}, bf16[12,1,8192]{2,0,1:T(8,128)(2,1)}, u32[]{:S(2)}) copy-start(bf16[12,1,8192]{2,0,1:T(8,128)(2,1)} %param.13) | copy-start | bytes 589828
  174.0 168.1 %all-to-all-start.1 = ((bf16[128,2,8192]{2,1,0:T(2,128)(2,1)}), bf16[128,2,8192]{2,1,0:T(2,128)(2,1)}, u32[]{:S(2)}, u32[]{:S(2)}) async-start(bf16[128,2,8192]{2,1,0:T(2,128)(2,1)} %reshape.131), calls=%async_computation.1 | async-start | bytes 8388608 | tf_op jit(solution)/shard_map/all_to_all | solution.py:261
  191.7 196.3 %reduce-scatter.2.cloned.1.call-start = ((), (), s32[]{:S(2)}) async-start(), calls=%async_computation.5 | async-start | bytes 983040 | tf_op jit(solution)/shard_map/reduce_scatter | solution.py:300
  192.6 131.6 %copy-start.4 = (bf16[1536,64]{0,1:T(8,128)(2,1)}, bf16[1536,64]{0,1:T(8,128)(2,1)S(1)}, u32[]{:S(2)}) copy-start(bf16[1536,64]{0,1:T(8,128)(2,1)S(1)} %copy.46) | copy-start | bytes 589828
  192.9 132.4 %copy-start.2 = (bf16[1536,192]{0,1:T(8,128)(2,1)}, bf16[1536,192]{0,1:T(8,128)(2,1)S(1)}, u32[]{:S(2)}) copy-start(bf16[1536,192]{0,1:T(8,128)(2,1)S(1)} %convolution_convert_fusion) | copy-start | bytes 1769476
  195.9 0.7 copy-start.9
  338.1 2.6 copy-start.5
  354.7 3.5 copy-start.1
  358.3 2.1 copy-start.7
  360.4 2.8 copy-start.8
Sparse Core Ops, SparseCore 0:
  10.1 37.3 all-gather.1
  342.2 17.0 reduce-scatter.1

commit v2 on v1

--- a/solution.py
+++ b/solution.py
@@ -1,5 +1,3 @@
-import functools
-
 import jax
 import jax.numpy as jnp
 from jax import lax
@@ -10,6 +8,8 @@
 epsilon = 1e-06
 HIGHEST = lax.Precision.HIGHEST
 SIDE = 8
+CAP = 2
+SUM_BYTES = 100_000_000
 
 
 def contract_rows(left, right):
@@ -142,8 +142,172 @@
         compiler_params=pltpu.CompilerParams(
             collective_id=collective_id, has_side_effects=True
         ),
+        cost_estimate=pl.CostEstimate(
+            flops=0, bytes_accessed=SUM_BYTES, transcendentals=0
+        ),
         name="sum_nodes",
     )(x)
+
+
+def pack(tile):
+    half = tile.shape[0] // 2
+    return jnp.concatenate([tile[:half], tile[half:]], axis=1)
+
+
+def unpack(tile):
+    half = tile.shape[1] // 2
+    return jnp.concatenate([tile[:, :half], tile[:, half:]], axis=0)
+
+
+def back_kernel(slot_ref, adj_ref, grad_ref, out_ref, terms, sem):
+    tiles, width = adj_ref.shape[0], adj_ref.shape[1]
+
+    def one_tile(t, carry):
+        grad = grad_ref[t]
+        for n in range(width):
+            term = lax.dot_general(
+                adj_ref[t, n], grad, (((0,), (0,)), ((), ())),
+                preferred_element_type=jnp.float32,
+            )
+            j = t * width + n
+            terms[j] = pack(term).astype(jnp.bfloat16)
+        return carry
+
+    lax.fori_loop(0, tiles, one_tile, 0)
+
+    def place(j, carry):
+        pltpu.make_async_copy(terms.at[j], out_ref.at[slot_ref[j]], sem).start()
+        return carry
+
+    lax.fori_loop(0, tiles * width, place, 0)
+    pltpu.make_async_copy(terms, out_ref.at[pl.ds(0, tiles * width)], sem).wait()
+
+
+def place_back_terms(slot_index, adj_all, grad_tiles, slots):
+    tiles, width = adj_all.shape[:2]
+    rows, columns = grad_tiles.shape[1:]
+    packed = (rows // 2, columns * 2)
+    return pl.pallas_call(
+        back_kernel,
+        out_shape=jax.ShapeDtypeStruct((slots,) + packed, jnp.bfloat16),
+        in_specs=[
+            pl.BlockSpec(memory_space=pltpu.SMEM),
+            pl.BlockSpec(memory_space=pltpu.VMEM),
+            pl.BlockSpec(memory_space=pltpu.VMEM),
+        ],
+        out_specs=pl.BlockSpec(memory_space=pl.ANY),
+        scratch_shapes=[
+            pltpu.VMEM((tiles * width,) + packed, jnp.bfloat16),
+            pltpu.SemaphoreType.DMA,
+        ],
+        name="place_back_terms",
+    )(slot_index, adj_all, grad_tiles)
+
+
+def pick_kernel(id_ref, y_ref, out_ref, packed_ref, sem):
+    for t in range(y_ref.shape[0]):
+        packed_ref[t] = pack(y_ref[t].astype(jnp.float32)).astype(jnp.bfloat16)
+
+    def place(j, carry):
+        pltpu.make_async_copy(packed_ref.at[id_ref[j]], out_ref.at[j], sem).start()
+        return carry
+
+    lax.fori_loop(0, out_ref.shape[0], place, 0)
+    pltpu.make_async_copy(out_ref, out_ref, sem).wait()
+
+
+def pick_tiles(ids, y_tiles):
+    tiles, rows, columns = y_tiles.shape
+    packed = (rows // 2, columns * 2)
+    return pl.pallas_call(
+        pick_kernel,
+        out_shape=jax.ShapeDtypeStruct((ids.shape[0],) + packed, jnp.bfloat16),
+        in_specs=[
+            pl.BlockSpec(memory_space=pltpu.SMEM),
+            pl.BlockSpec(memory_space=pltpu.VMEM),
+        ],
+        out_specs=pl.BlockSpec(memory_space=pl.ANY),
+        scratch_shapes=[
+            pltpu.VMEM((tiles,) + packed, jnp.bfloat16),
+            pltpu.SemaphoreType.DMA,
+        ],
+        name="pick_tiles",
+    )(ids, y_tiles)
+
+
+def add_kernel(id_ref, returned_ref, grad_ref, dy_ref, acc):
+    acc[...] = jnp.zeros_like(acc)
+
+    def add(j, carry):
+        tile = id_ref[j]
+
+        @pl.when(tile >= 0)
+        def _():
+            acc[tile] = acc[tile] + returned_ref[j].astype(jnp.float32)
+
+        return carry
+
+    lax.fori_loop(0, returned_ref.shape[0], add, 0)
+    for t in range(grad_ref.shape[0]):
+        total = grad_ref[t].astype(jnp.float32) + unpack(acc[t])
+        dy_ref[t] = total.astype(jnp.bfloat16)
+
+
+def add_returned(ids, returned, grad_tiles):
+    tiles, rows, columns = grad_tiles.shape
+    return pl.pallas_call(
+        add_kernel,
+        out_shape=jax.ShapeDtypeStruct(grad_tiles.shape, jnp.bfloat16),
+        in_specs=[
+            pl.BlockSpec(memory_space=pltpu.SMEM),
+            pl.BlockSpec(memory_space=pltpu.VMEM),
+            pl.BlockSpec(memory_space=pltpu.VMEM),
+        ],
+        out_specs=pl.BlockSpec(memory_space=pltpu.VMEM),
+        scratch_shapes=[pltpu.VMEM((tiles, rows // 2, columns * 2), jnp.float32)],
+        name="add_returned",
+    )(ids, returned, grad_tiles)
+
+
+def mixed_kernel(slot_ref, fetched_ref, adj_ref, base_ref, out_ref, held, sem):
+    tiles, width = adj_ref.shape[0], adj_ref.shape[1]
+
+    def fetch(j, carry):
+        pltpu.make_async_copy(fetched_ref.at[slot_ref[j]], held.at[j], sem).start()
+        return carry
+
+    lax.fori_loop(0, tiles * width, fetch, 0)
+    pltpu.make_async_copy(fetched_ref.at[pl.ds(0, tiles * width)], held, sem).wait()
+
+    def one_tile(t, carry):
+        acc = base_ref[t]
+        for n in range(width):
+            rows = unpack(held[t * width + n].astype(jnp.float32)).astype(jnp.bfloat16)
+            acc = acc + jnp.dot(adj_ref[t, n], rows, preferred_element_type=jnp.float32)
+        out_ref[t] = acc.astype(jnp.bfloat16)
+        return carry
+
+    lax.fori_loop(0, tiles, one_tile, 0)
+
+
+def finish_mixed(slot_index, fetched, adj_all, base):
+    tiles, width = adj_all.shape[:2]
+    return pl.pallas_call(
+        mixed_kernel,
+        out_shape=jax.ShapeDtypeStruct(base.shape, jnp.bfloat16),
+        in_specs=[
+            pl.BlockSpec(memory_space=pltpu.SMEM),
+            pl.BlockSpec(memory_space=pl.ANY),
+            pl.BlockSpec(memory_space=pltpu.VMEM),
+            pl.BlockSpec(memory_space=pltpu.VMEM),
+        ],
+        out_specs=pl.BlockSpec(memory_space=pltpu.VMEM),
+        scratch_shapes=[
+            pltpu.VMEM((tiles * width,) + fetched.shape[1:], jnp.bfloat16),
+            pltpu.SemaphoreType.DMA,
+        ],
+        name="finish_mixed",
+    )(slot_index, fetched, adj_all, base)
 
 
 def local(feats, w_qkv, w_gcn, nbr_owner, nbr_tile, adj_blocks, grad_out):
@@ -152,47 +316,28 @@
     head_width = w_gcn.shape[1]
     tile_rows_n = feats.shape[2] // head_width
     row_count = tile_count * tile_rows_n
+    node_count = lax.axis_size("nodes")
+    slots = node_count * CAP
+    entries = tile_count * list_width
+    total_rows = jnp.float32(row_count * node_count)
+    adj_all = lax.all_gather(adj_blocks, "feat", axis=1, tiled=True)
     gathered = lax.all_gather(feats, "feat", axis=1, tiled=True)
+    gathered, grad_out = lax.optimization_barrier((gathered, grad_out))
     head_count = gathered.shape[1]
     full_rows = (
         gathered.reshape(tile_count, head_count, tile_rows_n, head_width)
         .transpose(0, 2, 1, 3)
         .reshape(row_count, head_count * head_width)
     )
-    adj_all = lax.all_gather(adj_blocks, "feat", axis=1, tiled=True)
-    grad_rows = grad_out.reshape(row_count, head_width)
-    node_count = lax.axis_size("nodes")
-    slot_cap = max(2, (tile_count * list_width + node_count - 1) // node_count)
-    total_rows = jnp.float32(row_count * node_count)
+    grad_tiles = grad_out.reshape(tile_count, tile_rows_n, head_width)
+    grad_rows = grad_tiles.reshape(row_count, head_width)
 
     owners = nbr_owner.reshape(-1)
-    local_ids = nbr_tile.reshape(-1)
-    owner_hot = (owners[:, None] == jnp.arange(node_count, dtype=jnp.int32)[None, :]).astype(
-        jnp.int32
-    )
-    rank_within = jnp.sum((jnp.cumsum(owner_hot, axis=0) - owner_hot) * owner_hot, axis=1)
-    slot_index = owners * slot_cap + rank_within
-    request = jnp.zeros((node_count * slot_cap,), jnp.int32).at[slot_index].set(local_ids)
-    incoming = lax.all_to_all(
-        request.reshape(node_count, slot_cap), "nodes", split_axis=0, concat_axis=0, tiled=True
-    )
-    incoming_flat = incoming.reshape(-1)
-
-    grad_tiles = grad_rows.reshape(tile_count, tile_rows_n, head_width)
-    back_term = jnp.einsum(
-        "tnab,tah->tnbh", adj_all, grad_tiles, preferred_element_type=jnp.float32
-    ).astype(jnp.bfloat16)
-    outgoing = jnp.zeros((node_count * slot_cap, tile_rows_n * head_width), jnp.bfloat16)
-    outgoing = outgoing.at[slot_index].set(
-        back_term.reshape(tile_count * list_width, tile_rows_n * head_width)
-    )
-    returned = lax.all_to_all(
-        outgoing.reshape(node_count, slot_cap, tile_rows_n * head_width),
-        "nodes",
-        split_axis=0,
-        concat_axis=0,
-        tiled=True,
-    )
+    place = jnp.arange(entries, dtype=jnp.int32)
+    earlier = place[:, None] > place[None, :]
+    same = owners[:, None] == owners[None, :]
+    rank_within = jnp.sum((earlier & same).astype(jnp.int32), axis=1)
+    slot_index = owners * CAP + rank_within
 
     proj = jnp.dot(full_rows, w_qkv, preferred_element_type=jnp.float32).astype(jnp.bfloat16)
     query_rows = proj[:, :head_width]
@@ -217,16 +362,52 @@
         ],
         axis=0,
     )
+    codes = jnp.pad(
+        (nbr_owner * tile_count + nbr_tile).reshape(-1).astype(jnp.float32),
+        (0, lanes - entries),
+    )
+    own_row = jnp.arange(node_count, dtype=jnp.int32) == lax.axis_index("nodes")
+    own_list = jnp.where(own_row[:, None], codes[None, :], 0.0)
     sent = jnp.concatenate(
         [
             x_local[:, :lanes],
             x_local[:, lanes:],
             jnp.concatenate([kv_local, pq_local], axis=1),
             squares,
+            own_list,
         ],
         axis=0,
     )
     summed = sum_nodes(sent, 0)
+    summed, adj_all = lax.optimization_barrier((summed, adj_all))
+    outgoing = place_back_terms(slot_index, adj_all, grad_tiles, slots)
+    exchange_shape = (node_count, CAP) + outgoing.shape[1:]
+    returned = lax.all_to_all(
+        outgoing.reshape(exchange_shape), "nodes", split_axis=0, concat_axis=0, tiled=True
+    ).reshape(outgoing.shape)
+
+    listed = summed[2 * depth + lanes :, :entries].astype(jnp.int32)
+    wanted = listed // tile_count == lax.axis_index("nodes")
+    before = jnp.dot(
+        wanted.astype(jnp.bfloat16),
+        earlier.T.astype(jnp.bfloat16),
+        preferred_element_type=jnp.float32,
+    )
+    marked = jnp.where(wanted, listed % tile_count + 1, 0)
+    incoming = (
+        jnp.stack(
+            [jnp.sum(jnp.where(before == r, marked, 0), axis=1) for r in range(CAP)], axis=1
+        ).reshape(-1)
+        - 1
+    )
+
+    y_rows = jnp.dot(full_rows, w_gcn, preferred_element_type=jnp.float32).astype(jnp.bfloat16)
+    picked = pick_tiles(
+        jnp.maximum(incoming, 0), y_rows.reshape(tile_count, tile_rows_n, head_width)
+    )
+    fetched = lax.all_to_all(
+        picked.reshape(exchange_shape), "nodes", split_axis=0, concat_axis=0, tiled=True
+    ).reshape(outgoing.shape)
     x_query = summed[:depth, :head_width]
     x_key = summed[:depth, head_width:]
     x_value = summed[depth : 2 * depth, :head_width]
@@ -251,27 +432,8 @@
         axis=1,
     )
 
-    y_rows = jnp.dot(full_rows, w_gcn, preferred_element_type=jnp.float32).astype(jnp.bfloat16)
-    y_tiles = y_rows.reshape(tile_count, tile_rows_n * head_width)
-    picked = (
-        y_tiles.at[incoming_flat]
-        .get(mode="promise_in_bounds")
-        .reshape(node_count, slot_cap, tile_rows_n * head_width)
-    )
-    fetched = lax.all_to_all(picked, "nodes", split_axis=0, concat_axis=0, tiled=True)
-    neighbours = (
-        fetched.reshape(node_count * slot_cap, tile_rows_n * head_width)
-        .at[slot_index]
-        .get(mode="promise_in_bounds")
-    )
-    neighbours = neighbours.reshape(tile_count, list_width, tile_rows_n, head_width)
-    gcn_sum = jnp.einsum(
-        "tnab,tnbh->tah", adj_all, neighbours, preferred_element_type=jnp.float32
-    ).reshape(row_count, head_width)
     mix_rows = jnp.dot(query_full, kv_state, precision=HIGHEST)
-    mixed = (value_full + attn_scale * mix_rows + y_rows.astype(jnp.float32) + gcn_sum).astype(
-        jnp.bfloat16
-    )
+    base = value_full + attn_scale * mix_rows + y_rows.astype(jnp.float32)
     dq_rows = (
         attn_scale * jnp.dot(grad_full, kv_state.T, precision=HIGHEST)
         + 2.0 * gq_coef * query_full
@@ -280,13 +442,7 @@
     dv_rows = grad_full + jnp.dot(key_full, dm_state, precision=HIGHEST)
     dqkv = jnp.concatenate([dq_rows, dk_rows, dv_rows], axis=1).astype(jnp.bfloat16)
 
-    tile_hot = (incoming_flat[:, None] == jnp.arange(tile_count, dtype=jnp.int32)[None, :]).astype(
-        jnp.bfloat16
-    )
-    back_sum = contract_rows(
-        tile_hot, returned.reshape(node_count * slot_cap, tile_rows_n * head_width)
-    )
-    dy_rows = (grad_full + back_sum.reshape(row_count, head_width)).astype(jnp.bfloat16)
+    dy_rows = add_returned(incoming, returned, grad_tiles).reshape(row_count, head_width)
     gcn_local = contract_rows(full_rows, dy_rows)
     gcn_sent = jnp.concatenate([gcn_local[: depth // 2], gcn_local[depth // 2 :]], axis=1)
     gcn_summed = sum_nodes(gcn_sent, 1)
@@ -299,6 +455,9 @@
     )
     grad_x = lax.psum_scatter(
         partial_grad.astype(jnp.bfloat16), "feat", scatter_dimension=1, tiled=True
+    )
+    mixed = finish_mixed(
+        slot_index, fetched, adj_all, base.reshape(tile_count, tile_rows_n, head_width)
     )
     mixed_tiles = mixed.reshape(tile_count, 1, tile_rows_n * head_width)
     grad_x_tiles = grad_x.reshape(tile_count, 1, tile_rows_n * head_width)

time: 399 us -> 347 us (0.87)
  waiting for transfers between devices: 80.2 us -> 167 us
  local copies, waits for them, and re-layouts: 72.9 us -> 16.8 us
  Pallas kernels: 137 us -> 95.6 us
  starting transfers between devices: 51.3 us -> 25 us
  matrix products: 20.2 us -> 7.47 us
    all_to_all x3 -> x2, waiting for transfers between devices: 64.2 us -> 166 us  [the longest x1 89.9 us: local(): lax.all_to_all(outgoing.reshape(exchange_shape), 'nodes', split_axis=0, c...]
    pallas_call x2, Pallas kernels: 137 us -> 73.1 us  [sum_nodes(): pl.pallas_call(sum_kernel, out_shape=jax.ShapeDtypeStruct((rows, lanes),...]
    reshape x13 -> x2, local copies, waits for them, and re-layouts: 38.3 us -> 1.23 us  [the longest x1 1.15 us: local(): grad_tiles = grad_out.reshape(tile_count, tile_rows_n, head_width)]
    all_to_all x3 -> x2, starting transfers between devices: 51 us -> 24.8 us  [the longest x1 17.7 us: local(): lax.all_to_all(picked.reshape(exchange_shape), 'nodes', split_axis=0, con...]
    pallas_call x0 -> x4, Pallas kernels: none -> 22.5 us  [the longest x1 6.95 us: add_returned(): pl.pallas_call(add_kernel, out_shape=jax.ShapeDtypeStruct(grad_tiles.shap...]
    all_gather x1, waiting for transfers between devices: 15.3 us -> 0.01 us  [local(): adj_all = lax.all_gather(adj_blocks, 'feat', axis=1, tiled=True)]
    gather x2 -> x0, local copies, waits for them, and re-layouts: 10.5 us -> none  [the longest x1 5.38 us: local(): neighbours = fetched.reshape(node_count * slot_cap, tile_rows_n * head_wi...]
    scatter x2 -> x0, local copies, waits for them, and re-layouts: 5.09 us -> none  [the longest x1 4.37 us: local(): outgoing.at[slot_index]]
  transfers between devices with their start and end apart: 5 -> 4, of which waited for: 2 -> 2; matrix products, arithmetic and copies ran while one was open for 24% -> 7% of each run, Pallas kernels for 34% -> 26%
where the time goes in v2:
time: 347 us; the launch traced here: 346 us
  waiting for transfers between devices  167 us (48%)
  Pallas kernels  95.6 us (28%)
  starting transfers between devices  25 us (7%)
  between operations  17.8 us (5%)
  local copies, waits for them, and re-layouts  16.8 us (5%)
  blocking collectives  13.2 us (4%)
  matrix products  7.47 us (2%)
  other arithmetic  3.76 us (1%)
    all_to_all x1, waiting for transfers between devices, local(): lax.all_to_all(outgoing.reshape(exchange_shape), 'nodes', split_axis=0, c...  89.9 us
    all_to_all x1, waiting for transfers between devices, local(): lax.all_to_all(picked.reshape(exchange_shape), 'nodes', split_axis=0, con...  76.1 us
    pallas_call x2, Pallas kernels, sum_nodes(): pl.pallas_call(sum_kernel, out_shape=jax.ShapeDtypeStruct((rows, lanes),...  73.1 us
    all_to_all x1, starting transfers between devices, local(): lax.all_to_all(picked.reshape(exchange_shape), 'nodes', split_axis=0, con...  17.7 us
    all_gather x1, blocking collectives, local(): gathered = lax.all_gather(feats, 'feat', axis=1, tiled=True)  13.2 us
    all_to_all x1, starting transfers between devices, local(): lax.all_to_all(outgoing.reshape(exchange_shape), 'nodes', split_axis=0, c...  7.05 us
    pallas_call x1, Pallas kernels, add_returned(): pl.pallas_call(add_kernel, out_shape=jax.ShapeDtypeStruct(grad_tiles.shap...  6.95 us
  transfers between devices with their start and end apart: 4, of which 2 were waited for; matrix products, arithmetic and copies ran while one was open for 7% of the time, Pallas kernels for 26%

profile of v2, /device:TPU:1, one launch (start us, length us, event | category | flops | bytes accessed | tf_op | source)
XLA Modules:
  0.0 346.4 jit_solution(2672810666501673744)
XLA Ops:
  7.9 13.2 %all_gather.6 = bf16[12,4,8192]{2,0,1:T(8,128)(2,1)S(1)} all-gather(bf16[12,1,8192]{2,0,1:T(8,128)(2,1)} %param.7), channel_id=1, replica_groups=mesh['nodes'=128,'feat'=4] {'feat'}, dimensions={1}, use_global_device_ids=true | all-gather | bytes 983040 | tf_op jit(solution)/shard_map/all_gather | solution.py:324
  21.7 1.2 reshape.60
  23.0 1.1 copy.64
  25.0 1.1 reshape.67.grad_ref
  27.5 0.7 fusion.24
  29.7 0.7 copy-done.4
  30.4 42.9 %sum_nodes.2 = f32[768,128]{1,0:T(8,128)} custom-call(f32[768,128]{1,0:T(8,128)} %copy-done.4), custom_call_target="tpu_custom_call" | custom-call | bytes 100000000 | tf_op jit(solution)/shard_map/sum_nodes/pallas_call | solution.py:124
  74.1 5.9 %place_back_terms.1 = bf16[256,64,128]{2,1,0:T(8,128)(2,1)} custom-call(s32[48]{0:T(128)} %multiply_add_fusion.slot_ref, bf16[12,4,128,128]{3,2,1,0:T(8,128)(2,1)} %all-gather.2.cloned.1.call-done.adj_ref, bf16[12,128,64]{2,1,0:T(8,128)(2,1)} %reshape.67.grad_ref), custom_call_target="tpu_custom_call" | custom-call | tf_op jit(solution)/shard_map/place_back_terms/pallas_call | solution.py:190
  79.9 7.1 %all-to-all-start.1 = ((bf16[128,2,64,128]{3,2,1,0:T(8,128)(2,1)}), bf16[128,2,64,128]{3,2,1,0:T(8,128)(2,1)}, u32[]{:S(2)}, u32[]{:S(2)}) async-start(bf16[128,2,64,128]{3,2,1,0:T(8,128)(2,1)} %bitcast.38), calls=%async_computation.1 | async-start | bytes 8388608 | tf_op jit(solution)/shard_map/all_to_all | solution.py:385
  87.3 0.9 copy.70
  89.3 3.3 pick_tiles.1
  92.6 89.9 %all-to-all-done.1 = bf16[128,2,64,128]{3,2,1,0:T(8,128)(2,1)} async-done(((bf16[128,2,64,128]{3,2,1,0:T(8,128)(2,1)}), bf16[128,2,64,128]{3,2,1,0:T(8,128)(2,1)}, u32[]{:S(2)}, u32[]{:S(2)}) %all-to-all-start.1) | async-done | bytes 4194336 | tf_op jit(solution)/shard_map/all_to_all | solution.py:385
  182.5 17.7 %all-to-all-start = ((bf16[128,2,64,128]{3,2,1,0:T(8,128)(2,1)}), bf16[128,2,64,128]{3,2,1,0:T(8,128)(2,1)}, u32[]{:S(2)}, u32[]{:S(2)}) async-start(bf16[128,2,64,128]{3,2,1,0:T(8,128)(2,1)} %bitcast.37), calls=%async_computation | async-start | bytes 8388608 | tf_op jit(solution)/shard_map/all_to_all | solution.py:408
  207.3 6.9 %add_returned.1 = bf16[12,128,64]{2,1,0:T(8,128)(2,1)} custom-call(s32[256]{0:T(256)} %copy-done.6, bf16[256,64,128]{2,1,0:T(8,128)(2,1)} %bitcast.10.returned_ref, bf16[12,128,64]{2,1,0:T(8,128)(2,1)} %reshape.67.grad_ref), custom_call_target="tpu_custom_call" | custom-call | tf_op jit(solution)/shard_map/add_returned/pallas_call | solution.py:258
  214.2 2.3 fusion
  216.9 1.2 copy.71
  218.9 0.8 copy.79
  219.7 76.1 %all-to-all-done = bf16[128,2,64,128]{3,2,1,0:T(8,128)(2,1)} async-done(((bf16[128,2,64,128]{3,2,1,0:T(8,128)(2,1)}), bf16[128,2,64,128]{3,2,1,0:T(8,128)(2,1)}, u32[]{:S(2)}, u32[]{:S(2)}) %all-to-all-start) | async-done | bytes 4194336 | tf_op jit(solution)/shard_map/all_to_all | solution.py:408
  295.8 6.4 %finish_mixed.1 = bf16[12,128,64]{2,1,0:T(8,128)(2,1)} custom-call(s32[48]{0:T(128)} %multiply_add_fusion.slot_ref, bf16[256,64,128]{2,1,0:T(8,128)(2,1)} %bitcast.5.fetched_ref, bf16[12,4,128,128]{3,2,1,0:T(8,128)(2,1)} %all-gather.2.cloned.1.call-done.adj_ref, f32[12,128,64]{2,1,0:T(8,128)} %bitcast.44), custom_call_target="tpu_custom_call" | custom-call | tf_op jit(solution)/shard_map/finish_mixed/pallas_call | solution.py:295
  302.3 2.1 reshape.66
  305.4 30.2 %sum_nodes.3 = f32[128,128]{1,0:T(8,128)} custom-call(f32[128,128]{1,0:T(8,128)} %pad_maximum_fusion.2.x_ref), custom_call_target="tpu_custom_call" | custom-call | bytes 100000000 | tf_op jit(solution)/shard_map/sum_nodes/pallas_call | solution.py:124
  335.6 1.0 fusion.58
  337.3 1.1 copy.73
  338.5 1.0 reshape.71
  (67 shorter events, 13.5 us)
Async XLA Ops:
  7.2 16.9 %copy-start = (bf16[256,192]{0,1:T(8,128)(2,1)S(1)}, bf16[256,192]{0,1:T(8,128)(2,1)}, u32[]{:S(2)}) copy-start(bf16[256,192]{0,1:T(8,128)(2,1)} %param.8) | copy-start | bytes 294916
  7.2 66.9 %all-gather.2.cloned.1.call-start = ((), (), s32[]{:S(2)}) async-start(), calls=%async_computation.3 | async-start | bytes 1966080 | tf_op jit(solution)/shard_map/all_gather | solution.py:323
  22.9 1.5 copy-start.7
  23.0 1.5 copy-start.8
  23.0 1.6 copy-start.3
  29.6 0.8 copy-start.4
  79.9 7.1 %copy-start.5 = (bf16[256,64]{0,1:T(8,128)(2,1)S(1)}, bf16[256,64]{0,1:T(8,128)(2,1)}, u32[]{:S(2)}) copy-start(bf16[256,64]{0,1:T(8,128)(2,1)} %param.9) | copy-start | bytes 98308
  79.9 102.6 %all-to-all-start.1 = ((bf16[128,2,64,128]{3,2,1,0:T(8,128)(2,1)}), bf16[128,2,64,128]{3,2,1,0:T(8,128)(2,1)}, u32[]{:S(2)}, u32[]{:S(2)}) async-start(bf16[128,2,64,128]{3,2,1,0:T(8,128)(2,1)} %bitcast.38), calls=%async_computation.1 | async-start | bytes 8388608 | tf_op jit(solution)/shard_map/all_to_all | solution.py:385
  87.0 1.2 copy-start.1
  88.8 3.9 %copy-start.6 = (s32[256]{0:T(256)}, s32[256]{0:T(256)S(1)}, u32[]{:S(2)}) copy-start(s32[256]{0:T(256)S(1)} %sub.14.id_ref) | copy-start | bytes 3076
  182.5 113.3 %all-to-all-start = ((bf16[128,2,64,128]{3,2,1,0:T(8,128)(2,1)}), bf16[128,2,64,128]{3,2,1,0:T(8,128)(2,1)}, u32[]{:S(2)}, u32[]{:S(2)}) async-start(bf16[128,2,64,128]{3,2,1,0:T(8,128)(2,1)} %bitcast.37), calls=%async_computation | async-start | bytes 8388608 | tf_op jit(solution)/shard_map/all_to_all | solution.py:408
  200.3 137.1 %reduce-scatter.2.cloned.1.call-start = ((), (), s32[]{:S(2)}) async-start(), calls=%async_computation.4 | async-start | bytes 983040 | tf_op jit(solution)/shard_map/reduce_scatter | solution.py:456
  295.8 8.5 %copy-start.2 = (bf16[12,128,64]{2,1,0:T(8,128)(2,1)S(1)}, bf16[12,128,64]{2,1,0:T(8,128)(2,1)}, u32[]{:S(2)}) copy-start(bf16[12,128,64]{2,1,0:T(8,128)(2,1)} %add_returned.1) | copy-start | bytes 589828
Sparse Core Ops, SparseCore 0:
  10.1 37.3 all-gather.1
  216.7 27.8 reduce-scatter.1

commit v3 on v2

--- a/solution.py
+++ b/solution.py
@@ -173,7 +173,7 @@
             terms[j] = pack(term).astype(jnp.bfloat16)
         return carry
 
-    lax.fori_loop(0, tiles, one_tile, 0)
+    lax.fori_loop(0, tiles, one_tile, 0, unroll=4)
 
     def place(j, carry):
         pltpu.make_async_copy(terms.at[j], out_ref.at[slot_ref[j]], sem).start()
@@ -287,7 +287,7 @@
         out_ref[t] = acc.astype(jnp.bfloat16)
         return carry
 
-    lax.fori_loop(0, tiles, one_tile, 0)
+    lax.fori_loop(0, tiles, one_tile, 0, unroll=4)
 
 
 def finish_mixed(slot_index, fetched, adj_all, base):
@@ -355,25 +355,23 @@
     x_local = contract_rows(full_rows, stacked)
     depth = x_local.shape[0]
     lanes = 2 * head_width
-    squares = jnp.concatenate(
-        [
-            jnp.broadcast_to(sq_local, (head_width // 2, lanes)),
-            jnp.broadcast_to(sk_local, (head_width // 2, lanes)),
-        ],
-        axis=0,
-    )
+    me = lax.axis_index("nodes")
     codes = jnp.pad(
         (nbr_owner * tile_count + nbr_tile).reshape(-1).astype(jnp.float32),
-        (0, lanes - entries),
-    )
-    own_row = jnp.arange(node_count, dtype=jnp.int32) == lax.axis_index("nodes")
-    own_list = jnp.where(own_row[:, None], codes[None, :], 0.0)
+        (0, head_width - entries),
+    )
+    list_row = lax.broadcasted_iota(jnp.int32, (node_count // 2, lanes), 0)
+    list_lane = lax.broadcasted_iota(jnp.int32, (node_count // 2, lanes), 1)
+    mine = (list_row == me // 2) & (list_lane // head_width == me % 2)
+    own_list = jnp.where(mine, jnp.tile(codes, 2)[None, :], 0.0)
+    first = list_row == 0
+    own_list = own_list + jnp.where(first & (list_lane == entries), sq_local, 0.0)
+    own_list = own_list + jnp.where(first & (list_lane == entries + 1), sk_local, 0.0)
     sent = jnp.concatenate(
         [
             x_local[:, :lanes],
             x_local[:, lanes:],
             jnp.concatenate([kv_local, pq_local], axis=1),
-            squares,
             own_list,
         ],
         axis=0,
@@ -386,7 +384,12 @@
         outgoing.reshape(exchange_shape), "nodes", split_axis=0, concat_axis=0, tiled=True
     ).reshape(outgoing.shape)
 
-    listed = summed[2 * depth + lanes :, :entries].astype(jnp.int32)
+    lists = summed[2 * depth + head_width :]
+    listed = (
+        jnp.stack([lists[:, :entries], lists[:, head_width : head_width + entries]], axis=1)
+        .reshape(node_count, entries)
+        .astype(jnp.int32)
+    )
     wanted = listed // tile_count == lax.axis_index("nodes")
     before = jnp.dot(
         wanted.astype(jnp.bfloat16),
@@ -414,8 +417,8 @@
     x_grad = summed[depth : 2 * depth, head_width:]
     kv_state = summed[2 * depth : 2 * depth + head_width, :head_width]
     pq_state = summed[2 * depth : 2 * depth + head_width, head_width:]
-    sq_sum = summed[2 * depth + head_width, 0]
-    sk_sum = summed[2 * depth + head_width + head_width // 2, 0]
+    sq_sum = lists[0, entries]
+    sk_sum = lists[0, entries + 1]
     scale_grad = jnp.sum(pq_state * kv_state)
     attn_scale = jnp.sqrt(total_rows) / jnp.sqrt(sq_sum * sk_sum + epsilon)
     dm_state = attn_scale * pq_state
@@ -446,7 +449,6 @@
     gcn_local = contract_rows(full_rows, dy_rows)
     gcn_sent = jnp.concatenate([gcn_local[: depth // 2], gcn_local[depth // 2 :]], axis=1)
     gcn_summed = sum_nodes(gcn_sent, 1)
-    grad_gcn = jnp.concatenate([gcn_summed[:, :head_width], gcn_summed[:, head_width:]], axis=0)
     partial_grad = lax.dot_general(
         dqkv, w_qkv, (((1,), (1,)), ((), ())), preferred_element_type=jnp.float32
     )
@@ -456,9 +458,11 @@
     grad_x = lax.psum_scatter(
         partial_grad.astype(jnp.bfloat16), "feat", scatter_dimension=1, tiled=True
     )
+    base, gcn_summed = lax.optimization_barrier((base, gcn_summed))
     mixed = finish_mixed(
         slot_index, fetched, adj_all, base.reshape(tile_count, tile_rows_n, head_width)
     )
+    grad_gcn = jnp.concatenate([gcn_summed[:, :head_width], gcn_summed[:, head_width:]], axis=0)
     mixed_tiles = mixed.reshape(tile_count, 1, tile_rows_n * head_width)
     grad_x_tiles = grad_x.reshape(tile_count, 1, tile_rows_n * head_width)
     return (mixed_tiles, grad_x_tiles, grad_qkv, grad_gcn)

time: 347 us -> 335 us (0.965)
  waiting for transfers between devices: 167 us -> 90.1 us
  Pallas kernels: 95.6 us -> 155 us
    all_to_all x1, waiting for transfers between devices: 76.1 us -> 0.01 us  [local(): lax.all_to_all(picked.reshape(exchange_shape), 'nodes', split_axis=0, con...]
    pallas_call x2, Pallas kernels: 73.1 us -> 136 us  [sum_nodes(): pl.pallas_call(sum_kernel, out_shape=jax.ShapeDtypeStruct((rows, lanes),...]
  transfers between devices with their start and end apart: 4 -> 4, of which waited for: 2 -> 1; matrix products, arithmetic and copies ran while one was open for 7% -> 9% of each run, Pallas kernels for 26% -> 45%
where the time goes in v3:
time: 335 us; the launch traced here: 334 us
  Pallas kernels  155 us (46%)
  waiting for transfers between devices  90.1 us (27%)
  starting transfers between devices  25.6 us (8%)
  between operations  17.9 us (5%)
  local copies, waits for them, and re-layouts  17.8 us (5%)
  blocking collectives  13.2 us (4%)
  matrix products  9.1 us (3%)
  other arithmetic  5.93 us (2%)
    pallas_call x2, Pallas kernels, sum_nodes(): pl.pallas_call(sum_kernel, out_shape=jax.ShapeDtypeStruct((rows, lanes),...  136 us
    all_to_all x1, waiting for transfers between devices, local(): lax.all_to_all(outgoing.reshape(exchange_shape), 'nodes', split_axis=0, c...  89.4 us
    all_to_all x1, starting transfers between devices, local(): lax.all_to_all(picked.reshape(exchange_shape), 'nodes', split_axis=0, con...  17.7 us
    all_gather x1, blocking collectives, local(): gathered = lax.all_gather(feats, 'feat', axis=1, tiled=True)  13.2 us
    all_to_all x1, starting transfers between devices, local(): lax.all_to_all(outgoing.reshape(exchange_shape), 'nodes', split_axis=0, c...  7.66 us
    pallas_call x1, Pallas kernels, add_returned(): pl.pallas_call(add_kernel, out_shape=jax.ShapeDtypeStruct(grad_tiles.shap...  6.94 us
  transfers between devices with their start and end apart: 4, of which 1 were waited for; matrix products, arithmetic and copies ran while one was open for 9% of the time, Pallas kernels for 45%

profile of v3, /device:TPU:1, one launch (start us, length us, event | category | flops | bytes accessed | tf_op | source)
XLA Modules:
  0.0 334.4 jit_solution(3066516875404946755)
XLA Ops:
  7.9 13.2 %all_gather.6 = bf16[12,4,8192]{2,0,1:T(8,128)(2,1)S(1)} all-gather(bf16[12,1,8192]{2,0,1:T(8,128)(2,1)} %param.7), channel_id=1, replica_groups=mesh['nodes'=128,'feat'=4] {'feat'}, dimensions={1}, use_global_device_ids=true | all-gather | bytes 983040 | tf_op jit(solution)/shard_map/all_gather | solution.py:324
  21.5 1.1 reshape.71.grad_ref
  22.7 1.5 copy.104
  24.2 2.8 reshape.66
  27.0 1.1 copy.105
  29.8 1.4 select_add_fusion
  32.8 40.5 %sum_nodes.2 = f32[640,128]{1,0:T(8,128)} custom-call(f32[640,128]{1,0:T(8,128)} %pad_maximum_fusion.x_ref), custom_call_target="tpu_custom_call" | custom-call | bytes 100000000 | tf_op jit(solution)/shard_map/sum_nodes/pallas_call | solution.py:124
  74.2 3.7 %place_back_terms.1 = bf16[256,64,128]{2,1,0:T(8,128)(2,1)} custom-call(s32[48]{0:T(128)} %multiply_add_fusion.slot_ref, bf16[12,4,128,128]{3,2,1,0:T(8,128)(2,1)} %all-gather.2.cloned.1.call-done.adj_ref, bf16[12,128,64]{2,1,0:T(8,128)(2,1)} %reshape.71.grad_ref), custom_call_target="tpu_custom_call" | custom-call | tf_op jit(solution)/shard_map/place_back_terms/pallas_call | solution.py:190
  77.9 7.7 %all-to-all-start.1 = ((bf16[128,2,64,128]{3,2,1,0:T(8,128)(2,1)}), bf16[128,2,64,128]{3,2,1,0:T(8,128)(2,1)}, u32[]{:S(2)}, u32[]{:S(2)}) async-start(bf16[128,2,64,128]{3,2,1,0:T(8,128)(2,1)} %bitcast.44), calls=%async_computation.1 | async-start | bytes 8388608 | tf_op jit(solution)/shard_map/all_to_all | solution.py:383
  85.9 0.9 copy.119
  88.4 3.3 pick_tiles.1
  91.7 89.4 %all-to-all-done.1 = bf16[128,2,64,128]{3,2,1,0:T(8,128)(2,1)} async-done(((bf16[128,2,64,128]{3,2,1,0:T(8,128)(2,1)}), bf16[128,2,64,128]{3,2,1,0:T(8,128)(2,1)}, u32[]{:S(2)}, u32[]{:S(2)}) %all-to-all-start.1) | async-done | bytes 4194336 | tf_op jit(solution)/shard_map/all_to_all | solution.py:383
  181.1 17.7 %all-to-all-start = ((bf16[128,2,64,128]{3,2,1,0:T(8,128)(2,1)}), bf16[128,2,64,128]{3,2,1,0:T(8,128)(2,1)}, u32[]{:S(2)}, u32[]{:S(2)}) async-start(bf16[128,2,64,128]{3,2,1,0:T(8,128)(2,1)} %bitcast.43), calls=%async_computation | async-start | bytes 8388608 | tf_op jit(solution)/shard_map/all_to_all | solution.py:411
  203.8 1.0 fusion.7
  206.5 6.9 %add_returned.1 = bf16[12,128,64]{2,1,0:T(8,128)(2,1)} custom-call(s32[256]{0:T(256)} %copy-done.9, bf16[256,64,128]{2,1,0:T(8,128)(2,1)} %bitcast.13.returned_ref, bf16[12,128,64]{2,1,0:T(8,128)(2,1)} %reshape.71.grad_ref), custom_call_target="tpu_custom_call" | custom-call | tf_op jit(solution)/shard_map/add_returned/pallas_call | solution.py:258
  213.5 2.4 fusion
  217.5 1.4 fusion.2
  220.0 95.7 %sum_nodes.3 = f32[128,128]{1,0:T(8,128)} custom-call(f32[128,128]{1,0:T(8,128)} %pad_maximum_fusion.3.x_ref), custom_call_target="tpu_custom_call" | custom-call | bytes 100000000 | tf_op jit(solution)/shard_map/sum_nodes/pallas_call | solution.py:124
  315.8 1.0 fusion.60
  317.5 1.2 copy.122
  318.7 4.6 %finish_mixed.1 = bf16[12,128,64]{2,1,0:T(8,128)(2,1)} custom-call(s32[48]{0:T(128)} %multiply_add_fusion.slot_ref, bf16[256,64,128]{2,1,0:T(8,128)(2,1)} %bitcast.9.fetched_ref, bf16[12,4,128,128]{3,2,1,0:T(8,128)(2,1)} %all-gather.2.cloned.1.call-done.adj_ref, f32[12,128,64]{2,1,0:T(8,128)} %bitcast.50), custom_call_target="tpu_custom_call" | custom-call | tf_op jit(solution)/shard_map/finish_mixed/pallas_call | solution.py:295
  323.3 2.1 reshape.76
  325.3 1.1 copy.124
  326.5 1.0 reshape.77
  (85 shorter events, 13.7 us)
Async XLA Ops:
  7.2 21.5 %copy-start = (bf16[256,192]{0,1:T(8,128)(2,1)S(1)}, bf16[256,192]{0,1:T(8,128)(2,1)}, u32[]{:S(2)}) copy-start(bf16[256,192]{0,1:T(8,128)(2,1)} %param.8) | copy-start | bytes 294916
  7.2 13.9 %copy-start.6 = (bf16[12,1,8192]{2,0,1:T(8,128)(2,1)S(1)}, bf16[12,1,8192]{2,0,1:T(8,128)(2,1)}, u32[]{:S(2)}) copy-start(bf16[12,1,8192]{2,0,1:T(8,128)(2,1)} %param.13) | copy-start | bytes 589828
  7.2 67.0 %all-gather.2.cloned.1.call-start = ((), (), s32[]{:S(2)}) async-start(), calls=%async_computation.3 | async-start | bytes 1966080 | tf_op jit(solution)/shard_map/all_gather | solution.py:323
  26.9 1.1 copy-start.10
  26.9 1.2 copy-start.11
  29.0 176.5 %copy-start.1 = (bf16[1536,192]{0,1:T(8,128)(2,1)}, bf16[1536,192]{0,1:T(8,128)(2,1)S(1)}, u32[]{:S(2)}) copy-start(bf16[1536,192]{0,1:T(8,128)(2,1)S(1)} %convolution_convert_fusion) | copy-start | bytes 1769476
  77.9 7.7 %copy-start.8 = (bf16[256,64]{0,1:T(8,128)(2,1)S(1)}, bf16[256,64]{0,1:T(8,128)(2,1)}, u32[]{:S(2)}) copy-start(bf16[256,64]{0,1:T(8,128)(2,1)} %param.9) | copy-start | bytes 98308
  77.9 103.2 %all-to-all-start.1 = ((bf16[128,2,64,128]{3,2,1,0:T(8,128)(2,1)}), bf16[128,2,64,128]{3,2,1,0:T(8,128)(2,1)}, u32[]{:S(2)}, u32[]{:S(2)}) async-start(bf16[128,2,64,128]{3,2,1,0:T(8,128)(2,1)} %bitcast.44), calls=%async_computation.1 | async-start | bytes 8388608 | tf_op jit(solution)/shard_map/all_to_all | solution.py:383
  85.6 1.2 copy-start.2
  85.9 5.9 %copy-start.3 = (bf16[1536,64]{0,1:T(8,128)(2,1)}, bf16[1536,64]{0,1:T(8,128)(2,1)S(1)}, u32[]{:S(2)}) copy-start(bf16[1536,64]{0,1:T(8,128)(2,1)S(1)} %convolution_convert_fusion.1) | copy-start | bytes 589828
  87.9 3.9 %copy-start.9 = (s32[256]{0:T(256)}, s32[256]{0:T(256)S(1)}, u32[]{:S(2)}) copy-start(s32[256]{0:T(256)S(1)} %sub.27.id_ref) | copy-start | bytes 3076
  181.1 137.6 %all-to-all-start = ((bf16[128,2,64,128]{3,2,1,0:T(8,128)(2,1)}), bf16[128,2,64,128]{3,2,1,0:T(8,128)(2,1)}, u32[]{:S(2)}, u32[]{:S(2)}) async-start(bf16[128,2,64,128]{3,2,1,0:T(8,128)(2,1)} %bitcast.43), calls=%async_computation | async-start | bytes 8388608 | tf_op jit(solution)/shard_map/all_to_all | solution.py:411
  198.9 126.5 %reduce-scatter.2.cloned.1.call-start = ((), (), s32[]{:S(2)}) async-start(), calls=%async_computation.4 | async-start | bytes 983040 | tf_op jit(solution)/shard_map/reduce_scatter | solution.py:458
  213.4 3.1 copy-start.7
  215.8 1.7 copy-start.4
  215.8 3.1 copy-start.5
Sparse Core Ops, SparseCore 0:
  10.1 37.3 all-gather.1
  216.0 27.7 reduce-scatter.1

commit v4 on v3

--- a/solution.py
+++ b/solution.py
@@ -159,14 +159,15 @@
     return jnp.concatenate([tile[:, :half], tile[:, half:]], axis=0)
 
 
-def back_kernel(slot_ref, adj_ref, grad_ref, out_ref, terms, sem):
-    tiles, width = adj_ref.shape[0], adj_ref.shape[1]
+def back_kernel(slot_ref, grad_ref, *rest):
+    adj_refs, (out_ref, terms, sem) = rest[:-3], rest[-3:]
+    tiles, width = grad_ref.shape[0], len(adj_refs)
 
     def one_tile(t, carry):
         grad = grad_ref[t]
         for n in range(width):
             term = lax.dot_general(
-                adj_ref[t, n], grad, (((0,), (0,)), ((), ())),
+                adj_refs[n][t], grad, (((0,), (0,)), ((), ())),
                 preferred_element_type=jnp.float32,
             )
             j = t * width + n
@@ -184,8 +185,8 @@
 
 
 def place_back_terms(slot_index, adj_all, grad_tiles, slots):
-    tiles, width = adj_all.shape[:2]
-    rows, columns = grad_tiles.shape[1:]
+    width = len(adj_all)
+    tiles, rows, columns = grad_tiles.shape
     packed = (rows // 2, columns * 2)
     return pl.pallas_call(
         back_kernel,
@@ -193,15 +194,15 @@
         in_specs=[
             pl.BlockSpec(memory_space=pltpu.SMEM),
             pl.BlockSpec(memory_space=pltpu.VMEM),
-            pl.BlockSpec(memory_space=pltpu.VMEM),
-        ],
+        ]
+        + [pl.BlockSpec(memory_space=pltpu.VMEM)] * width,
         out_specs=pl.BlockSpec(memory_space=pl.ANY),
         scratch_shapes=[
             pltpu.VMEM((tiles * width,) + packed, jnp.bfloat16),
             pltpu.SemaphoreType.DMA,
         ],
         name="place_back_terms",
-    )(slot_index, adj_all, grad_tiles)
+    )(slot_index, grad_tiles, *adj_all)
 
 
 def pick_kernel(id_ref, y_ref, out_ref, packed_ref, sem):
@@ -269,8 +270,9 @@
     )(ids, returned, grad_tiles)
 
 
-def mixed_kernel(slot_ref, fetched_ref, adj_ref, base_ref, out_ref, held, sem):
-    tiles, width = adj_ref.shape[0], adj_ref.shape[1]
+def mixed_kernel(slot_ref, fetched_ref, base_ref, *rest):
+    adj_refs, (out_ref, held, sem) = rest[:-3], rest[-3:]
+    tiles, width = base_ref.shape[0], len(adj_refs)
 
     def fetch(j, carry):
         pltpu.make_async_copy(fetched_ref.at[slot_ref[j]], held.at[j], sem).start()
@@ -283,7 +285,7 @@
         acc = base_ref[t]
         for n in range(width):
             rows = unpack(held[t * width + n].astype(jnp.float32)).astype(jnp.bfloat16)
-            acc = acc + jnp.dot(adj_ref[t, n], rows, preferred_element_type=jnp.float32)
+            acc = acc + jnp.dot(adj_refs[n][t], rows, preferred_element_type=jnp.float32)
         out_ref[t] = acc.astype(jnp.bfloat16)
         return carry
 
@@ -291,7 +293,7 @@
 
 
 def finish_mixed(slot_index, fetched, adj_all, base):
-    tiles, width = adj_all.shape[:2]
+    tiles, width = base.shape[0], len(adj_all)
     return pl.pallas_call(
         mixed_kernel,
         out_shape=jax.ShapeDtypeStruct(base.shape, jnp.bfloat16),
@@ -299,15 +301,33 @@
             pl.BlockSpec(memory_space=pltpu.SMEM),
             pl.BlockSpec(memory_space=pl.ANY),
             pl.BlockSpec(memory_space=pltpu.VMEM),
-            pl.BlockSpec(memory_space=pltpu.VMEM),
-        ],
+        ]
+        + [pl.BlockSpec(memory_space=pltpu.VMEM)] * width,
         out_specs=pl.BlockSpec(memory_space=pltpu.VMEM),
         scratch_shapes=[
             pltpu.VMEM((tiles * width,) + fetched.shape[1:], jnp.bfloat16),
             pltpu.SemaphoreType.DMA,
         ],
         name="finish_mixed",
-    )(slot_index, fetched, adj_all, base)
+    )(slot_index, fetched, base, *adj_all)
+
+
+def shifted(block, shift):
+    count = lax.axis_size("feat")
+    return lax.ppermute(block, "feat", [(i, (i + shift) % count) for i in range(count)])
+
+
+def relative(rows):
+    count = lax.axis_size("feat")
+    size = rows.shape[0] // count
+    me = lax.axis_index("feat")
+    return jnp.concatenate(
+        [
+            lax.dynamic_slice_in_dim(rows, lax.rem(me - k + count, count) * size, size, axis=0)
+            for k in range(count)
+        ],
+        axis=0,
+    )
 
 
 def local(feats, w_qkv, w_gcn, nbr_owner, nbr_tile, adj_blocks, grad_out):
@@ -320,14 +340,17 @@
     slots = node_count * CAP
     entries = tile_count * list_width
     total_rows = jnp.float32(row_count * node_count)
-    adj_all = lax.all_gather(adj_blocks, "feat", axis=1, tiled=True)
-    gathered = lax.all_gather(feats, "feat", axis=1, tiled=True)
-    gathered, grad_out = lax.optimization_barrier((gathered, grad_out))
-    head_count = gathered.shape[1]
-    full_rows = (
-        gathered.reshape(tile_count, head_count, tile_rows_n, head_width)
-        .transpose(0, 2, 1, 3)
-        .reshape(row_count, head_count * head_width)
+    feat_count = lax.axis_size("feat")
+    w_qkv = relative(w_qkv)
+    w_gcn = relative(w_gcn)
+    own_feats = feats.reshape(tile_count, -1)
+    others = [shifted(own_feats, k) for k in range(1, feat_count)]
+    others, adj_own = lax.optimization_barrier(
+        (others, adj_blocks.reshape(tile_count, tile_rows_n, tile_rows_n))
+    )
+    adj_all = [adj_own] + [shifted(adj_own, k) for k in range(1, feat_count)]
+    full_rows = jnp.concatenate(
+        [block.reshape(row_count, head_width) for block in [own_feats] + others], axis=1
     )
     grad_tiles = grad_out.reshape(tile_count, tile_rows_n, head_width)
     grad_rows = grad_tiles.reshape(row_count, head_width)
@@ -337,7 +360,12 @@
     earlier = place[:, None] > place[None, :]
     same = owners[:, None] == owners[None, :]
     rank_within = jnp.sum((earlier & same).astype(jnp.int32), axis=1)
-    slot_index = owners * CAP + rank_within
+    slots_listed = (owners * CAP + rank_within).reshape(tile_count, list_width)
+    order = lax.rem(lax.axis_index("feat") - jnp.arange(list_width) + list_width, list_width)
+    picks = order[:, None] == jnp.arange(list_width)[None, :]
+    slot_index = jnp.sum(
+        jnp.where(picks[None], slots_listed[:, None, :], 0), axis=2
+    ).reshape(-1)
 
     proj = jnp.dot(full_rows, w_qkv, preferred_element_type=jnp.float32).astype(jnp.bfloat16)
     query_rows = proj[:, :head_width]
@@ -435,6 +463,7 @@
         axis=1,
     )
 
+    grad_qkv = relative(grad_qkv)
     mix_rows = jnp.dot(query_full, kv_state, precision=HIGHEST)
     base = value_full + attn_scale * mix_rows + y_rows.astype(jnp.float32)
     dq_rows = (
@@ -446,26 +475,32 @@
     dqkv = jnp.concatenate([dq_rows, dk_rows, dv_rows], axis=1).astype(jnp.bfloat16)
 
     dy_rows = add_returned(incoming, returned, grad_tiles).reshape(row_count, head_width)
-    gcn_local = contract_rows(full_rows, dy_rows)
+    gcn_local = relative(contract_rows(full_rows, dy_rows))
     gcn_sent = jnp.concatenate([gcn_local[: depth // 2], gcn_local[depth // 2 :]], axis=1)
-    gcn_summed = sum_nodes(gcn_sent, 1)
     partial_grad = lax.dot_general(
         dqkv, w_qkv, (((1,), (1,)), ((), ())), preferred_element_type=jnp.float32
     )
     partial_grad = partial_grad + lax.dot_general(
         dy_rows, w_gcn, (((1,), (1,)), ((), ())), preferred_element_type=jnp.float32
     )
-    grad_x = lax.psum_scatter(
-        partial_grad.astype(jnp.bfloat16), "feat", scatter_dimension=1, tiled=True
-    )
+    pieces = [
+        partial_grad[:, k * head_width : (k + 1) * head_width].astype(jnp.bfloat16)
+        for k in range(feat_count)
+    ]
+    grad_x = pieces[0].astype(jnp.float32)
+    for k in range(1, feat_count):
+        grad_x = grad_x + shifted(pieces[k], -k).astype(jnp.float32)
+    grad_x = grad_x.astype(jnp.bfloat16)
+    grad_x = grad_x.reshape(tile_count, 1, tile_rows_n * head_width)
+    grad_x, gcn_sent = lax.optimization_barrier((grad_x, gcn_sent))
+    gcn_summed = sum_nodes(gcn_sent, 1)
     base, gcn_summed = lax.optimization_barrier((base, gcn_summed))
     mixed = finish_mixed(
         slot_index, fetched, adj_all, base.reshape(tile_count, tile_rows_n, head_width)
     )
     grad_gcn = jnp.concatenate([gcn_summed[:, :head_width], gcn_summed[:, head_width:]], axis=0)
     mixed_tiles = mixed.reshape(tile_count, 1, tile_rows_n * head_width)
-    grad_x_tiles = grad_x.reshape(tile_count, 1, tile_rows_n * head_width)
-    return (mixed_tiles, grad_x_tiles, grad_qkv, grad_gcn)
+    return (mixed_tiles, grad_x, grad_qkv, grad_gcn)
 
 
 def solution(mesh):

time: 335 us -> 333 us (level)
  starting transfers between devices: 25.6 us -> 53.3 us
  Pallas kernels: 155 us -> 141 us
  blocking collectives: 13.2 us -> 0 us
  between operations: 17.9 us -> 4.94 us
  waiting for transfers between devices: 90.1 us -> 95.8 us
    ppermute x0 -> x9, starting transfers between devices: none -> 27.7 us  [shifted(): lax.ppermute(block, 'feat', [(i, (i + shift) % count) for i in range(coun...]
    pallas_call x2, Pallas kernels: 136 us -> 123 us  [sum_nodes(): pl.pallas_call(sum_kernel, out_shape=jax.ShapeDtypeStruct((rows, lanes),...]
    all_gather x1 -> x0, blocking collectives: 13.2 us -> none  [local(): gathered = lax.all_gather(feats, 'feat', axis=1, tiled=True)]
    ppermute x0 -> x9, waiting for transfers between devices: none -> 6.73 us  [shifted(): lax.ppermute(block, 'feat', [(i, (i + shift) % count) for i in range(coun...]
  transfers between devices with their start and end apart: 4 -> 11, of which waited for: 1 -> 3; matrix products, arithmetic and copies ran while one was open for 9% -> 8% of each run, Pallas kernels for 45% -> 40%
where the time goes in v4:
time: 333 us; the launch traced here: 331 us
  Pallas kernels  141 us (42%)
  waiting for transfers between devices  95.8 us (29%)
  starting transfers between devices  53.3 us (16%)
  local copies, waits for them, and re-layouts  20.3 us (6%)
  matrix products  8.58 us (3%)
  other arithmetic  7.24 us (2%)
  between operations  4.94 us (1%)
    pallas_call x2, Pallas kernels, sum_nodes(): pl.pallas_call(sum_kernel, out_shape=jax.ShapeDtypeStruct((rows, lanes),...  123 us
    all_to_all x1, waiting for transfers between devices, local(): lax.all_to_all(outgoing.reshape(exchange_shape), 'nodes', split_axis=0, c...  89.1 us
    ppermute x9, starting transfers between devices, shifted(): lax.ppermute(block, 'feat', [(i, (i + shift) % count) for i in range(coun...  27.7 us
    all_to_all x1, starting transfers between devices, local(): lax.all_to_all(picked.reshape(exchange_shape), 'nodes', split_axis=0, con...  17.7 us
    all_to_all x1, starting transfers between devices, local(): lax.all_to_all(outgoing.reshape(exchange_shape), 'nodes', split_axis=0, c...  7.87 us
    pallas_call x1, Pallas kernels, add_returned(): pl.pallas_call(add_kernel, out_shape=jax.ShapeDtypeStruct(grad_tiles.shap...  6.96 us
    ppermute x9, waiting for transfers between devices, shifted(): lax.ppermute(block, 'feat', [(i, (i + shift) % count) for i in range(coun...  6.73 us
  transfers between devices with their start and end apart: 11, of which 3 were waited for; matrix products, arithmetic and copies ran while one was open for 8% of the time, Pallas kernels for 40%

profile of v4, /device:TPU:1, one launch (start us, length us, event | category | flops | bytes accessed | tf_op | source)
XLA Modules:
  0.0 331.4 jit_solution(2225596001286235072)
XLA Ops:
  0.7 4.1 %collective-permute-start = (bf16[12,8192]{1,0:T(8,128)(2,1)}, bf16[12,8192]{1,0:T(8,128)(2,1)S(1)}, u32[]{:S(2)}, u32[]{:S(2)}) collective-permute-start(bf16[12,8192]{1,0:T(8,128)(2,1)} %bitcast.50), channel_id=1, source_target_pairs={{0,1},{1,2},{2,3},{3,0},{4,5},{5,6},{6,7},{7,4},{8,9},{9,10},{10,1... | collective-permute-start | bytes 589832 | tf_op jit(solution)/shard_map/ppermute | solution.py:317
  4.8 4.4 %collective-permute-start.1 = (bf16[12,8192]{1,0:T(8,128)(2,1)}, bf16[12,8192]{1,0:T(8,128)(2,1)S(1)}, u32[]{:S(2)}, u32[]{:S(2)}) collective-permute-start(bf16[12,8192]{1,0:T(8,128)(2,1)} %bitcast.51), channel_id=1, source_target_pairs={{0,2},{1,3},{2,0},{3,1},{4,6},{5,7},{6,4},{7,5},{8,10},{9,11},{10,... | collective-permute-start | bytes 589832 | tf_op jit(solution)/shard_map/ppermute | solution.py:317
  9.1 3.1 collective-permute-start.2
  12.2 1.4 reshape_reshape.6
  25.0 2.2 collective-permute-start.3
  27.2 2.8 collective-permute-start.4
  30.0 3.4 %collective-permute-start.5 = (bf16[12,128,128]{2,1,0:T(8,128)(2,1)S(1)}, bf16[12,128,128]{2,1,0:T(8,128)(2,1)S(1)}, u32[]{:S(2)}, u32[]{:S(2)}) collective-permute-start(bf16[12,128,128]{2,1,0:T(8,128)(2,1)S(1)} %bitcast.48), channel_id=1, source_target_pairs={{0,3},{1,0},{2,1},{3,2},{4,7},{5,4},{6,5},{7,6},{8,11},{9,8},{10,9... | collective-permute-start | bytes 1179656 | tf_op jit(solution)/shard_map/ppermute | solution.py:317
  36.3 41.8 %sum_nodes.2 = f32[640,128]{1,0:T(8,128)} custom-call(f32[640,128]{1,0:T(8,128)} %pad_maximum_fusion.1.x_ref), custom_call_target="tpu_custom_call" | custom-call | bytes 100000000 | tf_op jit(solution)/shard_map/sum_nodes/pallas_call | solution.py:124
  79.7 3.6 %place_back_terms.1 = bf16[256,64,128]{2,1,0:T(8,128)(2,1)} custom-call(s32[48]{0:T(128)} %reshape.111.slot_ref, bf16[12,128,64]{2,1,0:T(8,128)(2,1)} %reshape.120.grad_ref, bf16[12,128,128]{2,1,0:T(8,128)(2,1)} %bitcast.44, bf16[12,128,128]{2,1,0:T(8,128)(2,1)} %copy-done.3, bf16[12,128,128]{2,1,0:T(8,128)(2,1)} %copy-done.4, bf16[12,128,128]{2,1,0:T(8,128)(2,1)} %copy-done.5), custom_call_target="tpu_custom_call" | custom-call | tf_op jit(solution)/shard_map/place_back_terms/pallas_call | solution.py:191
  83.4 7.9 %all-to-all-start.1 = ((bf16[128,2,64,128]{3,2,1,0:T(8,128)(2,1)}), bf16[128,2,64,128]{3,2,1,0:T(8,128)(2,1)}, u32[]{:S(2)}, u32[]{:S(2)}) async-start(bf16[128,2,64,128]{3,2,1,0:T(8,128)(2,1)} %bitcast.40), calls=%async_computation.1 | async-start | bytes 8388608 | tf_op jit(solution)/shard_map/all_to_all | solution.py:411
  94.3 3.3 %pick_tiles.1 = bf16[256,64,128]{2,1,0:T(8,128)(2,1)} custom-call(s32[256]{0:T(256)} %broadcast_maximum_fusion.id_ref, bf16[12,128,64]{2,1,0:T(8,128)(2,1)} %bitcast.49), custom_call_target="tpu_custom_call" | custom-call | tf_op jit(solution)/shard_map/pick_tiles/pallas_call | solution.py:223
  97.7 89.1 %all-to-all-done.1 = bf16[128,2,64,128]{3,2,1,0:T(8,128)(2,1)} async-done(((bf16[128,2,64,128]{3,2,1,0:T(8,128)(2,1)}), bf16[128,2,64,128]{3,2,1,0:T(8,128)(2,1)}, u32[]{:S(2)}, u32[]{:S(2)}) %all-to-all-start.1) | async-done | bytes 4194336 | tf_op jit(solution)/shard_map/all_to_all | solution.py:411
  186.8 17.7 %all-to-all-start = ((bf16[128,2,64,128]{3,2,1,0:T(8,128)(2,1)}), bf16[128,2,64,128]{3,2,1,0:T(8,128)(2,1)}, u32[]{:S(2)}, u32[]{:S(2)}) async-start(bf16[128,2,64,128]{3,2,1,0:T(8,128)(2,1)} %bitcast.39), calls=%async_computation | async-start | bytes 8388608 | tf_op jit(solution)/shard_map/all_to_all | solution.py:439
  212.7 1.4 fusion.13
  215.3 7.0 %add_returned.1 = bf16[12,128,64]{2,1,0:T(8,128)(2,1)} custom-call(s32[256]{0:T(256)} %copy-done.22, bf16[256,64,128]{2,1,0:T(8,128)(2,1)} %bitcast.15.returned_ref, bf16[12,128,64]{2,1,0:T(8,128)(2,1)} %reshape.120.grad_ref), custom_call_target="tpu_custom_call" | custom-call | tf_op jit(solution)/shard_map/add_returned/pallas_call | solution.py:259
  222.2 1.5 fusion
  223.8 2.2 collective-permute-start.6
  226.1 3.6 %collective-permute-start.7 = (bf16[1536,64]{0,1:T(8,128)(2,1)S(1)}, bf16[1536,64]{0,1:T(8,128)(2,1)S(1)}, u32[]{:S(2)}, u32[]{:S(2)}) collective-permute-start(bf16[1536,64]{0,1:T(8,128)(2,1)S(1)} %get-tuple-element.52), channel_id=1, source_target_pairs={{0,2},{1,3},{2,0},{3,1},{4,6},{5,7},{6,4},{7,5},{8,10},{9,11},{10,... | collective-permute-start | bytes 589832 | tf_op jit(solution)/shard_map/ppermute | solution.py:317
  229.6 1.9 collective-permute-start.8
  232.7 1.8 collective-permute-done.7
  234.6 4.9 %collective-permute-done.8 = bf16[1536,64]{0,1:T(8,128)(2,1)S(1)} collective-permute-done((bf16[1536,64]{0,1:T(8,128)(2,1)S(1)}, bf16[1536,64]{0,1:T(8,128)(2,1)S(1)}, u32[]{:S(2)}, u32[]{:S(2)}) %collective-permute-start.8) | collective-permute-done | bytes 196640 | tf_op jit(solution)/shard_map/ppermute | solution.py:317
  240.8 81.0 %sum_nodes.3 = f32[128,128]{1,0:T(8,128)} custom-call(f32[128,128]{1,0:T(8,128)} %maximum_maximum_fusion.x_ref), custom_call_target="tpu_custom_call" | custom-call | bytes 100000000 | tf_op jit(solution)/shard_map/sum_nodes/pallas_call | solution.py:124
  324.8 4.6 %finish_mixed.1 = bf16[12,128,64]{2,1,0:T(8,128)(2,1)} custom-call(s32[48]{0:T(128)} %reshape.111.slot_ref, bf16[256,64,128]{2,1,0:T(8,128)(2,1)} %bitcast.10.fetched_ref, f32[12,128,64]{2,1,0:T(8,128)} %bitcast.43, bf16[12,128,128]{2,1,0:T(8,128)(2,1)} %bitcast.45, bf16[12,128,128]{2,1,0:T(8,128)(2,1)} %copy-done.3, bf16[12,128,128]{2,1,0:T(8,128)(2,1)} %copy-done.4, ...), custom_call_target="tpu_custom_call" | custom-call | tf_op jit(solution)/shard_map/finish_mixed/pallas_call | solution.py:297
  329.4 2.1 reshape.126
  (144 shorter events, 29.8 us)
Async XLA Ops:
  0.6 14.4 %copy-start.7 = (bf16[12,1,8192]{2,0,1:T(8,128)(2,1)S(1)}, bf16[12,1,8192]{2,0,1:T(8,128)(2,1)}, u32[]{:S(2)}) copy-start(bf16[12,1,8192]{2,0,1:T(8,128)(2,1)} %param.13) | copy-start | bytes 589828
  0.6 16.4 %copy-start.23 = (s32[12,4]{0,1:T(4,128)S(1)}, s32[12,4]{0,1:T(4,128)}, u32[]{:S(2)}) copy-start(s32[12,4]{0,1:T(4,128)} %param.10) | copy-start | bytes 580
  0.7 16.9 %copy-start.24 = (s32[12,4]{0,1:T(4,128)S(1)}, s32[12,4]{0,1:T(4,128)}, u32[]{:S(2)}) copy-start(s32[12,4]{0,1:T(4,128)} %param.11) | copy-start | bytes 580
  0.7 19.2 %copy-start.15 = (bf16[256,192]{0,1:T(8,128)(2,1)S(1)}, bf16[256,192]{0,1:T(8,128)(2,1)}, u32[]{:S(2)}) copy-start(bf16[256,192]{0,1:T(8,128)(2,1)} %param.8) | copy-start | bytes 294916
  0.7 19.4 %collective-permute-start = (bf16[12,8192]{1,0:T(8,128)(2,1)}, bf16[12,8192]{1,0:T(8,128)(2,1)S(1)}, u32[]{:S(2)}, u32[]{:S(2)}) collective-permute-start(bf16[12,8192]{1,0:T(8,128)(2,1)} %bitcast.50), channel_id=1, source_target_pairs={{0,1},{1,2},{2,3},{3,0},{4,5},{5,6},{6,7},{7,4},{8,9},{9,10},{10,1... | collective-permute-start | bytes 589832 | tf_op jit(solution)/shard_map/ppermute | solution.py:317
  4.8 15.3 %collective-permute-start.1 = (bf16[12,8192]{1,0:T(8,128)(2,1)}, bf16[12,8192]{1,0:T(8,128)(2,1)S(1)}, u32[]{:S(2)}, u32[]{:S(2)}) collective-permute-start(bf16[12,8192]{1,0:T(8,128)(2,1)} %bitcast.51), channel_id=1, source_target_pairs={{0,2},{1,3},{2,0},{3,1},{4,6},{5,7},{6,4},{7,5},{8,10},{9,11},{10,... | collective-permute-start | bytes 589832 | tf_op jit(solution)/shard_map/ppermute | solution.py:317
  9.1 11.0 %collective-permute-start.2 = (bf16[12,8192]{1,0:T(8,128)(2,1)}, bf16[12,8192]{1,0:T(8,128)(2,1)S(1)}, u32[]{:S(2)}, u32[]{:S(2)}) collective-permute-start(bf16[12,8192]{1,0:T(8,128)(2,1)} %bitcast.52), channel_id=1, source_target_pairs={{0,3},{1,0},{2,1},{3,2},{4,7},{5,4},{6,5},{7,6},{8,11},{9,8},{10,9... | collective-permute-start | bytes 589832 | tf_op jit(solution)/shard_map/ppermute | solution.py:317
  16.4 17.0 %copy-start.8 = (bf16[1536,64]{0,1:T(8,128)(2,1)}, bf16[1536,64]{0,1:T(8,128)(2,1)S(1)}, u32[]{:S(2)}) copy-start(bf16[1536,64]{0,1:T(8,128)(2,1)S(1)} %copy.86) | copy-start | bytes 589828
  24.9 9.0 %copy-start.25 = (pred[64]{0:T(512)(128)(4,1)S(1)}, pred[64]{0:T(512)(128)(4,1)}, u32[]{:S(2)}) copy-start(pred[64]{0:T(512)(128)(4,1)} %get-tuple-element.85) | copy-start | bytes 196
  24.9 9.0 %copy-start.26 = (pred[64]{0:T(512)(128)(4,1)S(1)}, pred[64]{0:T(512)(128)(4,1)}, u32[]{:S(2)}) copy-start(pred[64]{0:T(512)(128)(4,1)} %get-tuple-element.86) | copy-start | bytes 196
  24.9 9.0 %copy-start.27 = (f32[128]{0:T(128)S(1)}, f32[128]{0:T(128)}, u32[]{:S(2)}) copy-start(f32[128]{0:T(128)} %broadcast_in_dim.56) | copy-start | bytes 1540
  24.9 9.0 %copy-start.28 = (pred[128]{0:T(512)(128)(4,1)S(1)}, pred[128]{0:T(512)(128)(4,1)}, u32[]{:S(2)}) copy-start(pred[128]{0:T(512)(128)(4,1)} %iota_compare_fusion.4) | copy-start | bytes 388
  25.0 53.1 %collective-permute-start.3 = (bf16[12,128,128]{2,1,0:T(8,128)(2,1)S(1)}, bf16[12,128,128]{2,1,0:T(8,128)(2,1)S(1)}, u32[]{:S(2)}, u32[]{:S(2)}) collective-permute-start(bf16[12,128,128]{2,1,0:T(8,128)(2,1)S(1)} %bitcast.46), channel_id=1, source_target_pairs={{0,1},{1,2},{2,3},{3,0},{4,5},{5,6},{6,7},{7,4},{8,9},{9,10},{10,1... | collective-permute-start | bytes 1179656 | tf_op jit(solution)/shard_map/ppermute | solution.py:317
  27.2 50.9 %collective-permute-start.4 = (bf16[12,128,128]{2,1,0:T(8,128)(2,1)S(1)}, bf16[12,128,128]{2,1,0:T(8,128)(2,1)S(1)}, u32[]{:S(2)}, u32[]{:S(2)}) collective-permute-start(bf16[12,128,128]{2,1,0:T(8,128)(2,1)S(1)} %bitcast.47), channel_id=1, source_target_pairs={{0,2},{1,3},{2,0},{3,1},{4,6},{5,7},{6,4},{7,5},{8,10},{9,11},{10,... | collective-permute-start | bytes 1179656 | tf_op jit(solution)/shard_map/ppermute | solution.py:317
  30.0 48.1 %collective-permute-start.5 = (bf16[12,128,128]{2,1,0:T(8,128)(2,1)S(1)}, bf16[12,128,128]{2,1,0:T(8,128)(2,1)S(1)}, u32[]{:S(2)}, u32[]{:S(2)}) collective-permute-start(bf16[12,128,128]{2,1,0:T(8,128)(2,1)S(1)} %bitcast.48), channel_id=1, source_target_pairs={{0,3},{1,0},{2,1},{3,2},{4,7},{5,4},{6,5},{7,6},{8,11},{9,8},{10,9... | collective-permute-start | bytes 1179656 | tf_op jit(solution)/shard_map/ppermute | solution.py:317
  83.4 7.9 %copy-start.21 = (bf16[256,64]{0,1:T(8,128)(2,1)S(1)}, bf16[256,64]{0,1:T(8,128)(2,1)}, u32[]{:S(2)}) copy-start(bf16[256,64]{0,1:T(8,128)(2,1)} %param.9) | copy-start | bytes 98308
  83.4 103.4 %all-to-all-start.1 = ((bf16[128,2,64,128]{3,2,1,0:T(8,128)(2,1)}), bf16[128,2,64,128]{3,2,1,0:T(8,128)(2,1)}, u32[]{:S(2)}, u32[]{:S(2)}) async-start(bf16[128,2,64,128]{3,2,1,0:T(8,128)(2,1)} %bitcast.40), calls=%async_computation.1 | async-start | bytes 8388608 | tf_op jit(solution)/shard_map/all_to_all | solution.py:411
  186.8 138.0 %all-to-all-start = ((bf16[128,2,64,128]{3,2,1,0:T(8,128)(2,1)}), bf16[128,2,64,128]{3,2,1,0:T(8,128)(2,1)}, u32[]{:S(2)}, u32[]{:S(2)}) async-start(bf16[128,2,64,128]{3,2,1,0:T(8,128)(2,1)} %bitcast.39), calls=%async_computation | async-start | bytes 8388608 | tf_op jit(solution)/shard_map/all_to_all | solution.py:439
  215.3 7.0 %copy-start.20 = (bf16[64,64]{0,1:T(8,128)(2,1)S(1)}, bf16[64,64]{0,1:T(8,128)(2,1)}, u32[]{:S(2)}) copy-start(bf16[64,64]{0,1:T(8,128)(2,1)} %copy-done.19) | copy-start | bytes 24580
  222.2 9.3 %copy-start = (bf16[12,128,64]{2,1,0:T(8,128)(2,1)S(1)}, bf16[12,128,64]{2,1,0:T(8,128)(2,1)}, u32[]{:S(2)}) copy-start(bf16[12,128,64]{2,1,0:T(8,128)(2,1)} %add_returned.1) | copy-start | bytes 589828
  223.8 8.9 %collective-permute-start.6 = (bf16[1536,64]{0,1:T(8,128)(2,1)S(1)}, bf16[1536,64]{0,1:T(8,128)(2,1)S(1)}, u32[]{:S(2)}, u32[]{:S(2)}) collective-permute-start(bf16[1536,64]{0,1:T(8,128)(2,1)S(1)} %get-tuple-element.50), channel_id=1, source_target_pairs={{0,3},{1,0},{2,1},{3,2},{4,7},{5,4},{6,5},{7,6},{8,11},{9,8},{10,9... | collective-permute-start | bytes 589832 | tf_op jit(solution)/shard_map/ppermute | solution.py:317
  226.1 8.5 %collective-permute-start.7 = (bf16[1536,64]{0,1:T(8,128)(2,1)S(1)}, bf16[1536,64]{0,1:T(8,128)(2,1)S(1)}, u32[]{:S(2)}, u32[]{:S(2)}) collective-permute-start(bf16[1536,64]{0,1:T(8,128)(2,1)S(1)} %get-tuple-element.52), channel_id=1, source_target_pairs={{0,2},{1,3},{2,0},{3,1},{4,6},{5,7},{6,4},{7,5},{8,10},{9,11},{10,... | collective-permute-start | bytes 589832 | tf_op jit(solution)/shard_map/ppermute | solution.py:317
  229.6 9.8 %collective-permute-start.8 = (bf16[1536,64]{0,1:T(8,128)(2,1)S(1)}, bf16[1536,64]{0,1:T(8,128)(2,1)S(1)}, u32[]{:S(2)}, u32[]{:S(2)}) collective-permute-start(bf16[1536,64]{0,1:T(8,128)(2,1)S(1)} %get-tuple-element.51), channel_id=1, source_target_pairs={{0,1},{1,2},{2,3},{3,0},{4,5},{5,6},{6,7},{7,4},{8,9},{9,10},{10,1... | collective-permute-start | bytes 589832 | tf_op jit(solution)/shard_map/ppermute | solution.py:317
  232.7 90.8 %copy-start.6 = (f32[1536,64]{0,1:T(8,128)S(1)}, f32[1536,64]{0,1:T(8,128)}, u32[]{:S(2)}) copy-start(f32[1536,64]{0,1:T(8,128)} %fusion.2) | copy-start | bytes 1179652
  (16 other events, 47.6 us)

commit v5 on v4

--- a/solution.py
+++ b/solution.py
@@ -345,9 +345,7 @@
     w_gcn = relative(w_gcn)
     own_feats = feats.reshape(tile_count, -1)
     others = [shifted(own_feats, k) for k in range(1, feat_count)]
-    others, adj_own = lax.optimization_barrier(
-        (others, adj_blocks.reshape(tile_count, tile_rows_n, tile_rows_n))
-    )
+    adj_own = adj_blocks.reshape(tile_count, tile_rows_n, tile_rows_n)
     adj_all = [adj_own] + [shifted(adj_own, k) for k in range(1, feat_count)]
     full_rows = jnp.concatenate(
         [block.reshape(row_count, head_width) for block in [own_feats] + others], axis=1

time: 333 us -> 335 us (level)
  Pallas kernels: 141 us -> 137 us
  local copies, waits for them, and re-layouts: 20.3 us -> 23.7 us
    pallas_call x2, Pallas kernels: 123 us -> 119 us  [sum_nodes(): pl.pallas_call(sum_kernel, out_shape=jax.ShapeDtypeStruct((rows, lanes),...]
  transfers between devices with their start and end apart: 11 -> 11, of which waited for: 3 -> 3; matrix products, arithmetic and copies ran while one was open for 8% -> 11% of each run, Pallas kernels for 40% -> 39%
where the time goes in v5:
time: 335 us; the launch traced here: 334 us
  Pallas kernels  137 us (41%)
  waiting for transfers between devices  95.7 us (29%)
  starting transfers between devices  54.6 us (16%)
  local copies, waits for them, and re-layouts  23.7 us (7%)
  matrix products  9.48 us (3%)
  other arithmetic  8.46 us (3%)
  between operations  4.68 us (1%)
    pallas_call x2, Pallas kernels, sum_nodes(): pl.pallas_call(sum_kernel, out_shape=jax.ShapeDtypeStruct((rows, lanes),...  119 us
    all_to_all x1, waiting for transfers between devices, local(): lax.all_to_all(outgoing.reshape(exchange_shape), 'nodes', split_axis=0, c...  89.1 us
    ppermute x9, starting transfers between devices, shifted(): lax.ppermute(block, 'feat', [(i, (i + shift) % count) for i in range(coun...  29.1 us
    all_to_all x1, starting transfers between devices, local(): lax.all_to_all(picked.reshape(exchange_shape), 'nodes', split_axis=0, con...  17.7 us
    all_to_all x1, starting transfers between devices, local(): lax.all_to_all(outgoing.reshape(exchange_shape), 'nodes', split_axis=0, c...  7.71 us
    pallas_call x1, Pallas kernels, add_returned(): pl.pallas_call(add_kernel, out_shape=jax.ShapeDtypeStruct(grad_tiles.shap...  6.95 us
  transfers between devices with their start and end apart: 11, of which 3 were waited for; matrix products, arithmetic and copies ran while one was open for 11% of the time, Pallas kernels for 39%

profile of v5, /device:TPU:1, one launch (start us, length us, event | category | flops | bytes accessed | tf_op | source)
XLA Modules:
  0.0 334.0 jit_solution(10553053009039931276)
XLA Ops:
  0.7 4.1 %collective-permute-start = (bf16[12,8192]{1,0:T(8,128)(2,1)}, bf16[12,8192]{1,0:T(8,128)(2,1)}, u32[]{:S(2)}, u32[]{:S(2)}) collective-permute-start(bf16[12,8192]{1,0:T(8,128)(2,1)} %bitcast.50), channel_id=1, source_target_pairs={{0,1},{1,2},{2,3},{3,0},{4,5},{5,6},{6,7},{7,4},{8,9},{9,10},{10,1... | collective-permute-start | bytes 589832 | tf_op jit(solution)/shard_map/ppermute | solution.py:317
  4.8 4.4 %collective-permute-start.1 = (bf16[12,8192]{1,0:T(8,128)(2,1)}, bf16[12,8192]{1,0:T(8,128)(2,1)}, u32[]{:S(2)}, u32[]{:S(2)}) collective-permute-start(bf16[12,8192]{1,0:T(8,128)(2,1)} %bitcast.51), channel_id=1, source_target_pairs={{0,2},{1,3},{2,0},{3,1},{4,6},{5,7},{6,4},{7,5},{8,10},{9,11},{10,... | collective-permute-start | bytes 589832 | tf_op jit(solution)/shard_map/ppermute | solution.py:317
  9.1 3.1 collective-permute-start.2
  12.2 2.2 collective-permute-start.3
  14.4 2.8 collective-permute-start.4
  25.7 3.4 %collective-permute-start.5 = (bf16[12,128,128]{2,1,0:T(8,128)(2,1)S(1)}, bf16[12,128,128]{2,1,0:T(8,128)(2,1)S(1)}, u32[]{:S(2)}, u32[]{:S(2)}) collective-permute-start(bf16[12,128,128]{2,1,0:T(8,128)(2,1)S(1)} %bitcast.48), channel_id=1, source_target_pairs={{0,3},{1,0},{2,1},{3,2},{4,7},{5,4},{6,5},{7,6},{8,11},{9,8},{10,9... | collective-permute-start | bytes 1179656 | tf_op jit(solution)/shard_map/ppermute | solution.py:317
  29.2 2.1 reshape.113
  31.3 2.1 reshape.114
  34.6 1.7 pad_maximum_fusion
  41.6 39.2 %sum_nodes.2 = f32[640,128]{1,0:T(8,128)} custom-call(f32[640,128]{1,0:T(8,128)} %pad_maximum_fusion.1.x_ref), custom_call_target="tpu_custom_call" | custom-call | bytes 100000000 | tf_op jit(solution)/shard_map/sum_nodes/pallas_call | solution.py:124
  82.4 3.6 %place_back_terms.1 = bf16[256,64,128]{2,1,0:T(8,128)(2,1)} custom-call(s32[48]{0:T(128)} %reshape.111.slot_ref, bf16[12,128,64]{2,1,0:T(8,128)(2,1)} %reshape.120.grad_ref, bf16[12,128,128]{2,1,0:T(8,128)(2,1)} %bitcast.46, bf16[12,128,128]{2,1,0:T(8,128)(2,1)} %copy-done.3, bf16[12,128,128]{2,1,0:T(8,128)(2,1)} %copy-done.4, bf16[12,128,128]{2,1,0:T(8,128)(2,1)} %copy-done.5), custom_call_target="tpu_custom_call" | custom-call | tf_op jit(solution)/shard_map/place_back_terms/pallas_call | solution.py:191
  86.1 7.7 %all-to-all-start.1 = ((bf16[128,2,64,128]{3,2,1,0:T(8,128)(2,1)}), bf16[128,2,64,128]{3,2,1,0:T(8,128)(2,1)}, u32[]{:S(2)}, u32[]{:S(2)}) async-start(bf16[128,2,64,128]{3,2,1,0:T(8,128)(2,1)} %bitcast.40), calls=%async_computation.1 | async-start | bytes 8388608 | tf_op jit(solution)/shard_map/all_to_all | solution.py:409
  96.9 3.3 pick_tiles.1
  100.2 89.1 %all-to-all-done.1 = bf16[128,2,64,128]{3,2,1,0:T(8,128)(2,1)} async-done(((bf16[128,2,64,128]{3,2,1,0:T(8,128)(2,1)}), bf16[128,2,64,128]{3,2,1,0:T(8,128)(2,1)}, u32[]{:S(2)}, u32[]{:S(2)}) %all-to-all-start.1) | async-done | bytes 4194336 | tf_op jit(solution)/shard_map/all_to_all | solution.py:409
  189.3 17.7 %all-to-all-start = ((bf16[128,2,64,128]{3,2,1,0:T(8,128)(2,1)}), bf16[128,2,64,128]{3,2,1,0:T(8,128)(2,1)}, u32[]{:S(2)}, u32[]{:S(2)}) async-start(bf16[128,2,64,128]{3,2,1,0:T(8,128)(2,1)} %bitcast.39), calls=%async_computation | async-start | bytes 8388608 | tf_op jit(solution)/shard_map/all_to_all | solution.py:437
  217.7 7.0 %add_returned.1 = bf16[12,128,64]{2,1,0:T(8,128)(2,1)} custom-call(s32[256]{0:T(256)} %copy-done.17, bf16[256,64,128]{2,1,0:T(8,128)(2,1)} %bitcast.15.returned_ref, bf16[12,128,64]{2,1,0:T(8,128)(2,1)} %reshape.120.grad_ref), custom_call_target="tpu_custom_call" | custom-call | tf_op jit(solution)/shard_map/add_returned/pallas_call | solution.py:259
  224.7 1.5 fusion
  226.3 3.2 collective-permute-start.6
  229.5 3.2 collective-permute-start.7
  232.7 2.8 collective-permute-start.8
  238.0 5.3 %collective-permute-done.8 = bf16[1536,64]{0,1:T(8,128)(2,1)S(1)} collective-permute-done((bf16[1536,64]{0,1:T(8,128)(2,1)S(1)}, bf16[1536,64]{0,1:T(8,128)(2,1)S(1)}, u32[]{:S(2)}, u32[]{:S(2)}) %collective-permute-start.8) | collective-permute-done | bytes 196640 | tf_op jit(solution)/shard_map/ppermute | solution.py:317
  244.7 79.7 %sum_nodes.3 = f32[128,128]{1,0:T(8,128)} custom-call(f32[128,128]{1,0:T(8,128)} %maximum_maximum_fusion.x_ref), custom_call_target="tpu_custom_call" | custom-call | bytes 100000000 | tf_op jit(solution)/shard_map/sum_nodes/pallas_call | solution.py:124
  327.3 4.6 %finish_mixed.1 = bf16[12,128,64]{2,1,0:T(8,128)(2,1)} custom-call(s32[48]{0:T(128)} %reshape.111.slot_ref, bf16[256,64,128]{2,1,0:T(8,128)(2,1)} %bitcast.10.fetched_ref, f32[12,128,64]{2,1,0:T(8,128)} %bitcast.43, bf16[12,128,128]{2,1,0:T(8,128)(2,1)} %bitcast.47, bf16[12,128,128]{2,1,0:T(8,128)(2,1)} %copy-done.3, bf16[12,128,128]{2,1,0:T(8,128)(2,1)} %copy-done.4, ...), custom_call_target="tpu_custom_call" | custom-call | tf_op jit(solution)/shard_map/finish_mixed/pallas_call | solution.py:297
  331.9 2.1 reshape.126
  (134 shorter events, 33.4 us)
Async XLA Ops:
  0.6 19.5 %copy-start.7 = (bf16[12,1,8192]{2,0,1:T(8,128)(2,1)S(1)}, bf16[12,1,8192]{2,0,1:T(8,128)(2,1)}, u32[]{:S(2)}) copy-start(bf16[12,1,8192]{2,0,1:T(8,128)(2,1)} %param.13) | copy-start | bytes 589828
  0.6 21.5 %copy-start.18 = (s32[12,4]{0,1:T(4,128)S(1)}, s32[12,4]{0,1:T(4,128)}, u32[]{:S(2)}) copy-start(s32[12,4]{0,1:T(4,128)} %param.10) | copy-start | bytes 580
  0.7 22.0 %copy-start.19 = (s32[12,4]{0,1:T(4,128)S(1)}, s32[12,4]{0,1:T(4,128)}, u32[]{:S(2)}) copy-start(s32[12,4]{0,1:T(4,128)} %param.11) | copy-start | bytes 580
  0.7 24.3 %copy-start.11 = (bf16[256,192]{0,1:T(8,128)(2,1)S(1)}, bf16[256,192]{0,1:T(8,128)(2,1)}, u32[]{:S(2)}) copy-start(bf16[256,192]{0,1:T(8,128)(2,1)} %param.8) | copy-start | bytes 294916
  0.7 25.1 %collective-permute-start = (bf16[12,8192]{1,0:T(8,128)(2,1)}, bf16[12,8192]{1,0:T(8,128)(2,1)}, u32[]{:S(2)}, u32[]{:S(2)}) collective-permute-start(bf16[12,8192]{1,0:T(8,128)(2,1)} %bitcast.50), channel_id=1, source_target_pairs={{0,1},{1,2},{2,3},{3,0},{4,5},{5,6},{6,7},{7,4},{8,9},{9,10},{10,1... | collective-permute-start | bytes 589832 | tf_op jit(solution)/shard_map/ppermute | solution.py:317
  4.8 26.5 %collective-permute-start.1 = (bf16[12,8192]{1,0:T(8,128)(2,1)}, bf16[12,8192]{1,0:T(8,128)(2,1)}, u32[]{:S(2)}, u32[]{:S(2)}) collective-permute-start(bf16[12,8192]{1,0:T(8,128)(2,1)} %bitcast.51), channel_id=1, source_target_pairs={{0,2},{1,3},{2,0},{3,1},{4,6},{5,7},{6,4},{7,5},{8,10},{9,11},{10,... | collective-permute-start | bytes 589832 | tf_op jit(solution)/shard_map/ppermute | solution.py:317
  9.1 24.3 %collective-permute-start.2 = (bf16[12,8192]{1,0:T(8,128)(2,1)}, bf16[12,8192]{1,0:T(8,128)(2,1)S(1)}, u32[]{:S(2)}, u32[]{:S(2)}) collective-permute-start(bf16[12,8192]{1,0:T(8,128)(2,1)} %bitcast.52), channel_id=1, source_target_pairs={{0,3},{1,0},{2,1},{3,2},{4,7},{5,4},{6,5},{7,6},{8,11},{9,8},{10,9... | collective-permute-start | bytes 589832 | tf_op jit(solution)/shard_map/ppermute | solution.py:317
  12.2 68.6 %collective-permute-start.3 = (bf16[12,128,128]{2,1,0:T(8,128)(2,1)}, bf16[12,128,128]{2,1,0:T(8,128)(2,1)S(1)}, u32[]{:S(2)}, u32[]{:S(2)}) collective-permute-start(bf16[12,128,128]{2,1,0:T(8,128)(2,1)} %bitcast.44), channel_id=1, source_target_pairs={{0,1},{1,2},{2,3},{3,0},{4,5},{5,6},{6,7},{7,4},{8,9},{9,10},{10,1... | collective-permute-start | bytes 1179656 | tf_op jit(solution)/shard_map/ppermute | solution.py:317
  14.4 66.4 %collective-permute-start.4 = (bf16[12,128,128]{2,1,0:T(8,128)(2,1)}, bf16[12,128,128]{2,1,0:T(8,128)(2,1)S(1)}, u32[]{:S(2)}, u32[]{:S(2)}) collective-permute-start(bf16[12,128,128]{2,1,0:T(8,128)(2,1)} %bitcast.45), channel_id=1, source_target_pairs={{0,2},{1,3},{2,0},{3,1},{4,6},{5,7},{6,4},{7,5},{8,10},{9,11},{10,... | collective-permute-start | bytes 1179656 | tf_op jit(solution)/shard_map/ppermute | solution.py:317
  17.2 8.5 %copy-start.2 = (bf16[12,1,128,128]{3,2,1,0:T(8,128)(2,1)S(1)}, bf16[12,1,128,128]{3,2,1,0:T(8,128)(2,1)}, u32[]{:S(2)}) copy-start(bf16[12,1,128,128]{3,2,1,0:T(8,128)(2,1)} %param.12) | copy-start | bytes 1179652
  21.5 17.1 %copy-start.8 = (bf16[1536,64]{0,1:T(8,128)(2,1)}, bf16[1536,64]{0,1:T(8,128)(2,1)S(1)}, u32[]{:S(2)}) copy-start(bf16[1536,64]{0,1:T(8,128)(2,1)S(1)} %copy.86) | copy-start | bytes 589828
  25.7 55.1 %collective-permute-start.5 = (bf16[12,128,128]{2,1,0:T(8,128)(2,1)S(1)}, bf16[12,128,128]{2,1,0:T(8,128)(2,1)S(1)}, u32[]{:S(2)}, u32[]{:S(2)}) collective-permute-start(bf16[12,128,128]{2,1,0:T(8,128)(2,1)S(1)} %bitcast.48), channel_id=1, source_target_pairs={{0,3},{1,0},{2,1},{3,2},{4,7},{5,4},{6,5},{7,6},{8,11},{9,8},{10,9... | collective-permute-start | bytes 1179656 | tf_op jit(solution)/shard_map/ppermute | solution.py:317
  86.1 7.7 %copy-start.16 = (bf16[256,64]{0,1:T(8,128)(2,1)S(1)}, bf16[256,64]{0,1:T(8,128)(2,1)}, u32[]{:S(2)}) copy-start(bf16[256,64]{0,1:T(8,128)(2,1)} %param.9) | copy-start | bytes 98308
  86.1 103.3 %all-to-all-start.1 = ((bf16[128,2,64,128]{3,2,1,0:T(8,128)(2,1)}), bf16[128,2,64,128]{3,2,1,0:T(8,128)(2,1)}, u32[]{:S(2)}, u32[]{:S(2)}) async-start(bf16[128,2,64,128]{3,2,1,0:T(8,128)(2,1)} %bitcast.40), calls=%async_computation.1 | async-start | bytes 8388608 | tf_op jit(solution)/shard_map/all_to_all | solution.py:409
  93.9 6.3 %copy-start.12 = (bf16[64,64]{0,1:T(8,128)(2,1)}, bf16[64,64]{0,1:T(8,128)(2,1)S(1)}, u32[]{:S(2)}) copy-start(bf16[64,64]{0,1:T(8,128)(2,1)S(1)} %get-tuple-element.69) | copy-start | bytes 24580
  93.9 6.3 %copy-start.14 = (bf16[64,64]{0,1:T(8,128)(2,1)}, bf16[64,64]{0,1:T(8,128)(2,1)S(1)}, u32[]{:S(2)}) copy-start(bf16[64,64]{0,1:T(8,128)(2,1)S(1)} %get-tuple-element.70) | copy-start | bytes 24580
  189.3 138.0 %all-to-all-start = ((bf16[128,2,64,128]{3,2,1,0:T(8,128)(2,1)}), bf16[128,2,64,128]{3,2,1,0:T(8,128)(2,1)}, u32[]{:S(2)}, u32[]{:S(2)}) async-start(bf16[128,2,64,128]{3,2,1,0:T(8,128)(2,1)} %bitcast.39), calls=%async_computation | async-start | bytes 8388608 | tf_op jit(solution)/shard_map/all_to_all | solution.py:437
  217.7 7.0 %copy-start.13 = (bf16[64,64]{0,1:T(8,128)(2,1)S(1)}, bf16[64,64]{0,1:T(8,128)(2,1)}, u32[]{:S(2)}) copy-start(bf16[64,64]{0,1:T(8,128)(2,1)} %copy-done.12) | copy-start | bytes 24580
  217.7 7.0 %copy-start.15 = (bf16[64,64]{0,1:T(8,128)(2,1)S(1)}, bf16[64,64]{0,1:T(8,128)(2,1)}, u32[]{:S(2)}) copy-start(bf16[64,64]{0,1:T(8,128)(2,1)} %copy-done.14) | copy-start | bytes 24580
  224.7 10.8 %copy-start = (bf16[12,128,64]{2,1,0:T(8,128)(2,1)S(1)}, bf16[12,128,64]{2,1,0:T(8,128)(2,1)}, u32[]{:S(2)}) copy-start(bf16[12,128,64]{2,1,0:T(8,128)(2,1)} %add_returned.1) | copy-start | bytes 589828
  226.3 10.4 %collective-permute-start.6 = (bf16[1536,64]{0,1:T(8,128)(2,1)S(1)}, bf16[1536,64]{0,1:T(8,128)(2,1)S(1)}, u32[]{:S(2)}, u32[]{:S(2)}) collective-permute-start(bf16[1536,64]{0,1:T(8,128)(2,1)S(1)} %get-tuple-element.42), channel_id=1, source_target_pairs={{0,3},{1,0},{2,1},{3,2},{4,7},{5,4},{6,5},{7,6},{8,11},{9,8},{10,9... | collective-permute-start | bytes 589832 | tf_op jit(solution)/shard_map/ppermute | solution.py:317
  229.5 8.5 %collective-permute-start.7 = (bf16[1536,64]{0,1:T(8,128)(2,1)S(1)}, bf16[1536,64]{0,1:T(8,128)(2,1)S(1)}, u32[]{:S(2)}, u32[]{:S(2)}) collective-permute-start(bf16[1536,64]{0,1:T(8,128)(2,1)S(1)} %get-tuple-element.44), channel_id=1, source_target_pairs={{0,2},{1,3},{2,0},{3,1},{4,6},{5,7},{6,4},{7,5},{8,10},{9,11},{10,... | collective-permute-start | bytes 589832 | tf_op jit(solution)/shard_map/ppermute | solution.py:317
  232.7 10.6 %collective-permute-start.8 = (bf16[1536,64]{0,1:T(8,128)(2,1)S(1)}, bf16[1536,64]{0,1:T(8,128)(2,1)S(1)}, u32[]{:S(2)}, u32[]{:S(2)}) collective-permute-start(bf16[1536,64]{0,1:T(8,128)(2,1)S(1)} %get-tuple-element.43), channel_id=1, source_target_pairs={{0,1},{1,2},{2,3},{3,0},{4,5},{5,6},{6,7},{7,4},{8,9},{9,10},{10,1... | collective-permute-start | bytes 589832 | tf_op jit(solution)/shard_map/ppermute | solution.py:317
  236.7 89.4 %copy-start.6 = (f32[1536,64]{0,1:T(8,128)S(1)}, f32[1536,64]{0,1:T(8,128)}, u32[]{:S(2)}) copy-start(f32[1536,64]{0,1:T(8,128)} %fusion.2) | copy-start | bytes 1179652
  (11 other events, 14.7 us)
